TPU v7x, 256 devices: a whole 4x4x8 slice. The times are simulated.
256 devices in a mesh: pipe: 16 (over z, core), dp: 2 (over y_hi), tensor: 8 (over y_lo, x).
Axes of the slice: x: 4, y: 4 (y_hi: 2, y_lo: 2; y = y_hi * 2 + y_lo), z: 8, core: 2. Of those that a mesh axis runs over, the one named last changes fastest.
Arguments:
- ssm_output: bfloat16 [16, 2, 1024, 8192], P('pipe', 'dp', None, 'tensor'), may hold values from -6 to 6
- out_weight: bfloat16 [16, 8192, 4096], P('pipe', 'tensor', 'dp'), may hold values from -0.0625 to 0.0625
- in_weight: bfloat16 [16, 4096, 2048], P('pipe', 'dp', 'tensor'), may hold values from -0.09375 to 0.09375
- gain: float32 [16, 4096], P('pipe'), may hold values from 0.1 to 1.9
- residual: bfloat16 [16, 2, 1024, 4096], P('pipe', 'dp', 'tensor'), may hold values from -1.5 to 1.5
- proj_cotangent: bfloat16 [16, 2, 1024, 2048], P('pipe', 'dp', None, 'tensor'), may hold values from -6 to 6
- stream_cotangent: bfloat16 [16, 2, 1024, 4096], P('pipe', 'dp', 'tensor'), may hold values from -12 to 12
Outputs:
- stream: bfloat16 [16, 2, 1024, 4096], P('pipe', 'dp', 'tensor')
- b_proj: bfloat16 [16, 2, 1024, 2048], P('pipe', 'dp', None, 'tensor')
- residual_grad: bfloat16 [16, 2, 1024, 4096], P('pipe', 'dp', 'tensor')
- gain_grad: float32 [16, 4096], P('pipe')
All inputs are finite; a program needn't handle non-finite values.
Results may differ from a plain program's by a relative error of at most 0.014.
Values may be sent and summed in bfloat16 or wider, within the bound.
No kernel may reach another device: no remote copies, remote signals or barrier semaphores. Data moves between devices by JAX's collectives and lax.ppermute only.
A program may use at most 128 MiB of HBM per device.

v0:
```python
import math

import jax
import jax.numpy as jnp
from jax import lax
from jax.sharding import PartitionSpec as P

LAYERS = 118


def shifted(block, axis, distance):
    devices = range(lax.axis_size(axis))
    route = [((i - distance) % len(devices), i) for i in devices]
    return lax.ppermute(block, axis, route)


def body(ssm_output, out_weight, in_weight, gain, residual, proj_cotangent, stream_cotangent):
    depth_scale = 1.0 / math.sqrt(2.0 * LAYERS)
    out_all, in_all = (
        lax.all_gather(out_weight, "dp", axis=2, tiled=True),
        lax.all_gather(in_weight, "dp", axis=1, tiled=True),
    )
    w_out = out_all[0]
    w_in = in_all[0]
    ssm_rows = ssm_output[0]
    gain_row = gain[0]
    resid_rows = residual[0]
    cot_proj = proj_cotangent[0]
    cot_stream = stream_cotangent[0]
    block = ssm_rows
    mixed_sum = jnp.transpose(
        lax.psum_scatter(
            jnp.einsum("mtc,cd->tmd", block, w_out, preferred_element_type=jnp.float32).astype(
                jnp.bfloat16
            ),
            "tensor",
            scatter_dimension=0,
            tiled=True,
        ).astype(jnp.float32),
        (1, 0, 2),
    )
    own_stream = (resid_rows.astype(jnp.float32) + depth_scale * mixed_sum).astype(jnp.bfloat16)
    stream_rows = shifted(own_stream, "pipe", 1)
    stream_f32 = stream_rows.astype(jnp.float32)
    inv_rms = lax.rsqrt(jnp.mean(stream_f32 * stream_f32, axis=-1, keepdims=True) + 1e-05)
    unit_rows = stream_f32 * inv_rms
    normed = (unit_rows * gain_row).astype(jnp.bfloat16)
    projected = jnp.einsum(
        "mtd,dc->mtc",
        lax.all_gather(normed, "tensor", axis=1, tiled=True),
        w_in,
        preferred_element_type=jnp.float32,
    ).astype(jnp.bfloat16)
    block = cot_proj
    normed_grad = jnp.transpose(
        lax.psum_scatter(
            jnp.einsum("mtc,dc->tmd", block, w_in, preferred_element_type=jnp.float32).astype(
                jnp.bfloat16
            ),
            "tensor",
            scatter_dimension=0,
            tiled=True,
        ).astype(jnp.float32),
        (1, 0, 2),
    )
    gain_part = jnp.sum(normed_grad * unit_rows, axis=(0, 1))
    weighted = gain_row * normed_grad
    centre = jnp.mean(weighted * unit_rows, axis=-1, keepdims=True)
    stream_grad = (
        cot_stream.astype(jnp.float32) + inv_rms * (weighted - unit_rows * centre)
    ).astype(jnp.bfloat16)
    resid_grad = shifted(stream_grad, "pipe", -1)
    stream_rows, projected, resid_grad, gain_part = (stream_rows, projected, resid_grad, gain_part)
    gain_total = lax.psum(gain_part, ("dp", "tensor"))
    return (stream_rows[None], projected[None], resid_grad[None], gain_total[None])


def solution(mesh):
    in_specs = (
        P("pipe", "dp", None, "tensor"),
        P("pipe", "tensor", "dp"),
        P("pipe", "dp", "tensor"),
        P("pipe", None),
        P("pipe", "dp", "tensor", None),
        P("pipe", "dp", None, "tensor"),
        P("pipe", "dp", "tensor", None),
    )
    out_specs = (
        P("pipe", "dp", "tensor", None),
        P("pipe", "dp", None, "tensor"),
        P("pipe", "dp", "tensor", None),
        P("pipe", None),
    )
    return jax.shard_map(body, mesh=mesh, in_specs=in_specs, out_specs=out_specs, check_vma=False)
```

profile of v0, /device:TPU:16, one launch (start us, length us, event | category | flops | bytes accessed | tf_op | source)
XLA Modules:
  0.0 476.5 jit_solution(3154818368560495863)
XLA Ops:
  7.2 0.7 all-gather.4.cloned.1.call-update
  8.0 0.7 all-gather.8.cloned.1.call-update
  8.7 111.8 %all-gather.4.cloned.1.call-done = bf16[1,1024,4096]{2,1,0:T(8,128)(2,1)} async-done(((bf16[1,1024,2048]{2,1,0:T(8,128)(2,1)}), bf16[1,1024,4096]{2,1,0:T(8,128)(2,1)}) %all-gather.4.cloned.1.call-update) | async-done | bytes 8388624 | tf_op jit(solution)/shard_map/all_gather | solution.py:20
  120.5 14.6 %convert_bitcast_fusion.1 = bf16[1024,4096]{0,1:T(8,128)(2,1)} fusion(bf16[1,1024,4096]{2,1,0:T(8,128)(2,1)} %all-gather.4.cloned.1.call-done, bf16[1,1,1024,1024]{3,2,1,0:T(8,128)(2,1)S(1)} %copy-done), kind=kOutput, calls=%fused_computation.5 | convolution fusion | flops 8594128896 | bytes 18874368 | tf_op jit(solution)/shard_map/mtc,cd->tmd/dot_general | solution.py:33
  135.1 11.8 %copy.23 = bf16[1024,4096]{1,0:T(8,128)(2,1)} copy(bf16[1024,4096]{0,1:T(8,128)(2,1)} %convert_bitcast_fusion.1) | data formatting | bytes 16777216
  147.0 14.5 %all-gather.8.cloned.1.call-done = bf16[1,4096,256]{2,1,0:T(8,128)(2,1)} async-done(((bf16[1,2048,256]{2,1,0:T(8,128)(2,1)}), bf16[1,4096,256]{2,1,0:T(8,128)(2,1)}) %all-gather.8.cloned.1.call-update) | async-done | bytes 2097168 | tf_op jit(solution)/shard_map/all_gather | solution.py:21
  161.5 7.2 %convert_bitcast_fusion = bf16[1024,4096]{0,1:T(8,128)(2,1)} fusion(bf16[1,4096,256]{2,1,0:T(8,128)(2,1)} %all-gather.8.cloned.1.call-done, bf16[1,1,1024,256]{3,2,1,0:T(8,128)(2,1)S(1)} %copy-done.3), kind=kOutput, calls=%fused_computation.4 | convolution fusion | flops 2151677952 | bytes 11010048 | tf_op jit(solution)/shard_map/mtc,dc->tmd/dot_general | solution.py:57
  168.7 11.6 %copy.25 = bf16[1024,4096]{1,0:T(8,128)(2,1)} copy(bf16[1024,4096]{0,1:T(8,128)(2,1)} %convert_bitcast_fusion) | data formatting | bytes 16777216
  180.3 1.1 copy-done.2
  181.4 0.7 copy.15
  182.1 79.0 %reduce-scatter.7.cloned.1.call-done = bf16[128,4096]{1,0:T(8,128)(2,1)} async-done(((bf16[1024,4096]{1,0:T(8,128)(2,1)}), bf16[128,4096]{1,0:T(8,128)(2,1)}) %reduce-scatter.7.cloned.1.call-update) | async-done | bytes 1048592
  261.1 1.6 copy.24
  262.7 1.3 fusion.17
  264.0 1.6 copy.16
  265.7 91.9 %reduce-scatter.9.cloned.1.call-done = bf16[128,4096]{1,0:T(8,128)(2,1)} async-done(((bf16[1024,4096]{1,0:T(8,128)(2,1)}), bf16[128,4096]{1,0:T(8,128)(2,1)}) %reduce-scatter.9.cloned.1.call-update) | async-done | bytes 1048592
  357.6 1.6 copy.26
  359.8 1.4 fusion.16
  361.2 1.9 fusion.12
  363.2 2.7 collective-permute-start.1
  365.9 1.3 copy.17
  367.2 62.7 %psum.7 = f32[1,4096]{1,0:T(1,128)} all-reduce(f32[1,4096]{1,0:T(1,128)S(1)} %bitcast.68), channel_id=1, replica_groups=mesh['pipe'=16,'dp'=2,'tensor'=8] {'dp','tensor'}, use_global_device_ids=true, to_apply=%region_5.0 | all-reduce | flops 4096 | bytes 32768 | tf_op jit(solution)/shard_map/psum | solution.py:74
  429.9 1.3 copy.18
  431.2 31.5 %all-gather.6.cloned.1.call-done = bf16[1,1024,4096]{1,2,0:T(8,128)(2,1)} async-done(((bf16[1,128,4096]{1,2,0:T(8,128)(2,1)}), bf16[1,1024,4096]{1,2,0:T(8,128)(2,1)}) %all-gather.6.cloned.1.call-update) | async-done | bytes 8388624 | tf_op jit(solution)/shard_map/all_gather | solution.py:50
  462.7 7.3 %fusion.26 = bf16[1,1,1024,256]{3,2,1,0:T(8,128)(2,1)} fusion(bf16[1,4096,256]{2,1,0:T(8,128)(2,1)} %all-gather.8.cloned.1.call-done, bf16[1,1024,4096]{1,2,0:T(8,128)(2,1)} %all-gather.6.cloned.1.call-done), kind=kOutput, calls=%fused_computation.27 | convolution fusion | flops 2147745792 | bytes 11010048 | tf_op jit(solution)/shard_map/mtd,dc->mtc/dot_general | solution.py:48
  (23 shorter events, 0.9 us)
Async XLA Ops:
  7.2 113.3 %copy-start = (bf16[1,1,1024,1024]{3,2,1,0:T(8,128)(2,1)S(1)}, bf16[1,1,1024,1024]{3,2,1,0:T(8,128)(2,1)}, u32[]{:S(2)}) copy-start(bf16[1,1,1024,1024]{3,2,1,0:T(8,128)(2,1)} %param.7) | copy-start | bytes 6291460
  7.2 113.3 %all-gather.4.cloned.1.call-start = ((), (), s32[]{:S(2)}) async-start(), calls=%async_computation.2 | async-start | bytes 12582912 | tf_op jit(solution)/shard_map/all_gather | solution.py:20
  7.9 153.5 %all-gather.8.cloned.1.call-start = ((), (), s32[]{:S(2)}) async-start(), calls=%async_computation.4 | async-start | bytes 3145728 | tf_op jit(solution)/shard_map/all_gather | solution.py:21
  8.7 252.4 %reduce-scatter.7.cloned.1.call-start = ((), (), s32[]{:S(2)}) async-start(), calls=%async_computation.5 | async-start | bytes 9437184
  146.9 14.5 %copy-start.3 = (bf16[1,1,1024,256]{3,2,1,0:T(8,128)(2,1)S(1)}, bf16[1,1,1024,256]{3,2,1,0:T(8,128)(2,1)}, u32[]{:S(2)}) copy-start(bf16[1,1,1024,256]{3,2,1,0:T(8,128)(2,1)} %param.12) | copy-start | bytes 1572868
  147.0 210.7 %reduce-scatter.9.cloned.1.call-start = ((), (), s32[]{:S(2)}) async-start(), calls=%async_computation.6 | async-start | bytes 9437184
  180.2 1.2 copy-start.2
  180.2 282.4 %all-gather.6.cloned.1.call-start = ((), (), s32[]{:S(2)}) async-start(), calls=%async_computation.3 | async-start | bytes 9437184 | tf_op jit(solution)/shard_map/all_gather | solution.py:50
  264.0 95.2 %collective-permute-start = (bf16[1,128,4096]{1,2,0:T(8,128)(2,1)}, bf16[1,128,4096]{1,2,0:T(8,128)(2,1)S(1)}, u32[]{:S(2)}, u32[]{:S(2)}) collective-permute-start(bf16[1,128,4096]{1,2,0:T(8,128)(2,1)} %fusion.17), channel_id=1, source_target_pairs={{240,0},{0,16},{16,32},{32,48},{48,64},{64,80},{80,96},{96,112},{1... | collective-permute-start | bytes 3145736 | tf_op jit(solution)/shard_map/ppermute | solution.py:14
  265.7 94.1 %copy-start.4 = (f32[1,4096]{1,0:T(1,128)S(1)}, f32[1,4096]{1,0:T(1,128)}, u32[]{:S(2)}) copy-start(f32[1,4096]{1,0:T(1,128)} %param.10) | copy-start | bytes 49156
  363.2 66.7 %collective-permute-start.1 = (bf16[1,128,4096]{1,2,0:T(8,128)(2,1)}, bf16[1,128,4096]{1,2,0:T(8,128)(2,1)S(1)}, u32[]{:S(2)}, u32[]{:S(2)}) collective-permute-start(bf16[1,128,4096]{1,2,0:T(8,128)(2,1)} %get-tuple-element.14), channel_id=1, source_target_pairs={{16,0},{32,16},{48,32},{64,48},{80,64},{96,80},{112,96},{128,112},... | collective-permute-start | bytes 3145736 | tf_op jit(solution)/shard_map/ppermute | solution.py:14
  462.7 7.3 %copy-start.1 = (bf16[1,1,1024,1024]{3,2,1,0:T(8,128)(2,1)S(1)}, bf16[1,1,1024,1024]{3,2,1,0:T(8,128)(2,1)}, u32[]{:S(2)}) copy-start(bf16[1,1,1024,1024]{3,2,1,0:T(8,128)(2,1)} %param.7) | copy-start | bytes 6291460
Sparse Core Ops, SparseCore 0:
  9.8 110.6 all-gather.3
  122.3 39.1 all-gather.7
  164.0 97.0 reduce-scatter.6
  263.5 94.0 reduce-scatter.8
  363.3 99.3 all-gather.5
where the time goes:
time: 477 us
  waiting for transfers between devices  330 us (69%)
  blocking collectives  62.7 us (13%)
  local copies, waits for them, and re-layouts  32.7 us (7%)
  matrix products  29.1 us (6%)
  between operations  13.9 us (3%)
  other arithmetic  5.19 us (1%)
    unnamed x7, waiting for transfers between devices  172 us
    all_gather x1, waiting for transfers between devices, body(): lax.all_gather(out_weight, 'dp', axis=2, tiled=True)  112 us
    psum x1, blocking collectives, body(): gain_total = lax.psum(gain_part, ('dp', 'tensor'))  62.7 us
    unnamed x18, local copies, waits for them, and re-layouts  32.7 us
    all_gather x1, waiting for transfers between devices, body(): lax.all_gather(normed, 'tensor', axis=1, tiled=True)  31.5 us
    dot_general x1, matrix products, body(): jnp.einsum('mtc,cd->tmd', block, w_out, preferred_element_type=jnp.float32)  14.6 us
    all_gather x1, waiting for transfers between devices, body(): lax.all_gather(in_weight, 'dp', axis=1, tiled=True)  14.5 us
  transfers between devices with their start and end apart: 7, of which 5 were waited for; matrix products, arithmetic and copies ran while one was open for 11% of the time, Pallas kernels for 0%

commit v1 on v0

v1 whole, which is shorter than its diff:
```python
import math

import jax
import jax.numpy as jnp
from jax import lax
from jax.experimental import pallas as pl
from jax.experimental.pallas import tpu as pltpu
from jax.sharding import PartitionSpec as P


LAYERS = 118
NX = 4
NY = 4


PLANE = ("dp", "tensor")
ALL = ("pipe", "dp", "tensor")
f32 = jnp.float32
bf16 = jnp.bfloat16
shape = jax.ShapeDtypeStruct


def plane_route(to):
    return [
        (y * NX + x, (to(y, x)[0] % NY) * NX + to(y, x)[1] % NX)
        for y in range(NY)
        for x in range(NX)
    ]


RIGHT = plane_route(lambda y, x: (y, x + 1))
LEFT = plane_route(lambda y, x: (y, x - 1))
ACROSS = plane_route(lambda y, x: (y, x + 2))
PAIR = plane_route(lambda y, x: (y ^ 1, x))
CROSS = plane_route(lambda y, x: (3 - y, x))
REPLICA = plane_route(lambda y, x: (y + 2, x))
STAY = plane_route(lambda y, x: (y, x))


def move(block, route):
    return lax.ppermute(block, PLANE, route)


def ahead(block, route, distance=1):
    pipes = lax.axis_size("pipe")
    plane = NX * NY
    full = [
        (s * plane + a, ((s + distance) % pipes) * plane + b)
        for s in range(pipes)
        for a, b in route
    ]
    return lax.ppermute(block, ALL, full)


def after(block, *others):
    return lax.optimization_barrier((block, *others))[0]


def dot(a, b):
    return jnp.dot(a, b, preferred_element_type=f32)


def dot_t(a, b):
    return lax.dot_general(a, b, (((1,), (1,)), ((), ())), preferred_element_type=f32)


VMEM = pl.BlockSpec(memory_space=pltpu.VMEM)
SMEM = pl.BlockSpec(memory_space=pltpu.SMEM)


def run(kernel, out_shape, flops, moved, index, *args, scratch=()):
    count = len(out_shape) if isinstance(out_shape, list) else 1
    return pl.pallas_call(
        kernel,
        out_shape=out_shape,
        in_specs=[SMEM] + [VMEM] * len(args),
        out_specs=[VMEM] * count if count > 1 else VMEM,
        scratch_shapes=scratch,
        cost_estimate=pl.CostEstimate(flops=flops, bytes_accessed=moved, transcendentals=0),
        compiler_params=pltpu.CompilerParams(vmem_limit_bytes=24 << 20),
    )(index, *args)


HBM = pl.BlockSpec(memory_space=pltpu.HBM)


def load(parts, out_shape, index, arrays):
    def kernel(at, *refs):
        sources, outs, sems = refs[: len(arrays)], refs[len(arrays) : -1], refs[-1]
        copies = [
            pltpu.make_async_copy(a, b, sems.at[i])
            for i, (a, b) in enumerate(zip(parts(at, sources), outs))
        ]
        for copy in copies:
            copy.start()
        for copy in copies:
            copy.wait()

    return pl.pallas_call(
        kernel,
        out_shape=[shape(dims, bf16) for dims in out_shape],
        in_specs=[SMEM] + [HBM] * len(arrays),
        out_specs=[VMEM] * len(out_shape),
        scratch_shapes=[pltpu.SemaphoreType.DMA((len(out_shape),))],
        cost_estimate=pl.CostEstimate(
            flops=0, bytes_accessed=sum(4 * a.size for a in arrays), transcendentals=0
        ),
        compiler_params=pltpu.CompilerParams(vmem_limit_bytes=24 << 20),
    )(index, *arrays)


def add_terms(index, terms, dtype):
    def kernel(at, *refs):
        values = [ref[...].astype(f32) for ref in refs[:-1]]
        while len(values) > 1:
            values = [a + b for a, b in zip(values[::2], values[1::2])]
        refs[-1][...] = values[0].astype(dtype)

    return run(
        kernel, shape(terms[0].shape, dtype), terms[0].size, 8 * terms[0].size, index, *terms
    )


def back_products(index, cot, cot_pair, jobs):
    tokens = cot.shape[2]
    rows = jobs[0][1][0].shape[0]
    deep = min(256, rows)
    operands, plan = [], []
    for step, mine, theirs, adds, dtype in jobs:
        spots = []
        for array in (*mine, *theirs, *adds):
            known = [i for i, o in enumerate(operands) if o is array]
            if not known:
                operands.append(array)
            spots.append(known[0] if known else len(operands) - 1)
        plan.append((step, spots, dtype))

    def kernel(at, cot_ref, pair_ref, *refs):
        outs = refs[len(operands) :]
        for (step, spots, dtype), out in zip(plan, outs):
            a, b = cot_ref[at[4], at[step]], pair_ref[at[step]]
            for i in range(2):

                @pl.loop(0, rows // deep)
                def _(n):
                    own = pl.ds(pl.multiple_of(n * deep, deep), deep)
                    cols = pl.ds(pl.multiple_of(i * rows + n * deep, deep), deep)
                    value = dot_t(a, refs[spots[i]][own]) + dot_t(b, refs[spots[2 + i]][own])
                    for spot in spots[4:]:
                        value = value + refs[spot][:, cols].astype(f32)
                    out[:, cols] = value.astype(dtype)


    return run(
        kernel,
        [shape((tokens, 2 * rows), dtype) for _, _, dtype in plan],
        len(jobs) * 8 * tokens * cot.shape[3] * rows,
        sum(4 * o.size for o in operands),
        index,
        cot,
        cot_pair,
        *operands,
    )


def store(block):
    def kernel(block_ref, out_ref, sem):
        copy = pltpu.make_async_copy(block_ref, out_ref, sem)
        copy.start()
        copy.wait()

    return pl.pallas_call(
        kernel,
        out_shape=shape(block.shape, block.dtype),
        in_specs=[VMEM],
        out_specs=pl.BlockSpec(memory_space=pl.ANY),
        scratch_shapes=[pltpu.SemaphoreType.DMA],
        cost_estimate=pl.CostEstimate(flops=0, bytes_accessed=4 * block.size, transcendentals=0),
        compiler_params=pltpu.CompilerParams(vmem_limit_bytes=12 << 20),
        name="st",
    )(block)


def row_products(part, rows, steps, index, w, adds, choose=False):
    tokens, channels = part[0].shape[-2:]
    columns = w.shape[1]
    wide = min(512, columns)
    first = len(adds[0])

    def kernel(at, one_ref, two_ref, w_ref, *rest):
        add_refs, (p_ref, q_ref, both) = rest[:-3], rest[-3:]
        both[:tokens] = one_ref[at[steps[0]]]
        both[tokens:] = two_ref[at[steps[1]]]

        def step(n):
            cols = pl.ds(pl.multiple_of(n * wide, wide), wide)
            product = dot(both[...], w_ref[:, cols])
            p, q = product[:tokens], product[tokens:]
            for ref in add_refs[:first]:
                p = p + ref[:, cols].astype(f32)
            for ref in add_refs[first:]:
                q = q + ref[:, cols].astype(f32)
            if choose:
                swap = at[4] != 0
                p, q = jnp.where(swap, q, p), jnp.where(swap, p, q)
            p_ref[:, cols] = p.astype(bf16)
            q_ref[:, cols] = q.astype(bf16)

        pl.loop(0, columns // wide)(step)

    extra = list(adds[0]) + list(adds[1])
    return run(
        kernel,
        [shape((tokens, columns), bf16)] * 2,
        4 * tokens * channels * columns,
        2 * channels * columns + 4 * tokens * (channels + columns),
        index,
        part[rows[0]],
        part[rows[1]],
        w,
        *extra,
        scratch=[pltpu.VMEM((2 * tokens, channels), bf16)],
    )


def stream_and_norm(index, resid, keep, passed, crossed, gain, depth_scale):
    tokens, width = resid.shape
    half = width // 2
    rows = min(16, tokens)

    def kernel(at, r_ref, k_ref, p_ref, c_ref, g_ref, s_ref, nd, no, inv_ref):
        to_d = pl.ds(pl.multiple_of(at[5] * half, half), half)
        to_o = pl.ds(pl.multiple_of(at[6] * half, half), half)

        @pl.loop(0, tokens // rows)
        def _(n):
            r = pl.ds(pl.multiple_of(n * rows, rows), rows)
            sd = k_ref[r].astype(f32) + p_ref[r].astype(f32)
            sd = (r_ref[r, to_d].astype(f32) + depth_scale * sd).astype(bf16)
            so = (r_ref[r, to_o].astype(f32) + depth_scale * c_ref[r].astype(f32)).astype(bf16)
            s_ref[r, to_d] = sd
            s_ref[r, to_o] = so
            sd, so = sd.astype(f32), so.astype(f32)
            square = jnp.sum(sd * sd + so * so, axis=-1, keepdims=True)
            inv = lax.rsqrt(square / width + 1e-05)
            inv_ref[r] = inv
            nd[r] = (sd * inv * g_ref[:, to_d]).astype(bf16)
            no[r] = (so * inv * g_ref[:, to_o]).astype(bf16)

    return run(
        kernel,
        [
            shape((tokens, width), bf16),
            shape((tokens, half), bf16),
            shape((tokens, half), bf16),
            shape((tokens, 1), f32),
        ],
        12 * tokens * width,
        8 * tokens * width,
        index,
        resid,
        keep,
        passed,
        crossed,
        gain,
    )


def norm_backward(index, stream, inv, cot, gain, grad_d, grad_o):
    tokens, width = stream.shape
    half = width // 2
    rows = min(16, tokens)

    def kernel(at, s_ref, inv_ref, c_ref, g_ref, h0, h1, h2, h3, h4, h5, out, total):
        to_d = pl.ds(pl.multiple_of(at[5] * half, half), half)
        to_o = pl.ds(pl.multiple_of(at[6] * half, half), half)
        total[...] = jnp.zeros_like(total)

        @pl.loop(0, tokens // rows)
        def _(n):
            r = pl.ds(pl.multiple_of(n * rows, rows), rows)
            inv = inv_ref[r]
            hd = h0[r] + h1[r].astype(f32) + h2[r].astype(f32)
            ho = h3[r] + h4[r].astype(f32) + h5[r].astype(f32)
            ud, uo = s_ref[r, to_d].astype(f32) * inv, s_ref[r, to_o].astype(f32) * inv
            wd, wo = g_ref[:, to_d] * hd, g_ref[:, to_o] * ho
            centre = jnp.sum(wd * ud + wo * uo, axis=-1, keepdims=True) / width
            out[r, to_d] = (c_ref[r, to_d].astype(f32) + inv * (wd - ud * centre)).astype(bf16)
            out[r, to_o] = (c_ref[r, to_o].astype(f32) + inv * (wo - uo * centre)).astype(bf16)
            total[:, to_d] += jnp.sum(hd * ud, axis=0, keepdims=True)
            total[:, to_o] += jnp.sum(ho * uo, axis=0, keepdims=True)

    return run(
        kernel,
        [shape((tokens, width), bf16), shape((1, width), f32)],
        16 * tokens * width,
        16 * tokens * width,
        index,
        stream,
        inv,
        cot,
        gain,
        *grad_d,
        *grad_o,
    )


def project(index, blocks, weights):
    count = len(blocks)
    tokens, half = blocks[0][0].shape
    rows, columns = weights[0].shape

    def kernel(at, *refs):
        w, (mine, send), held = refs[2 * count : -3], refs[-3:-1], refs[-1]
        for i in range(count):
            held[i, 0] = refs[2 * i][...]
            held[i, 1] = refs[2 * i + 1][...]

        @pl.loop(0, count)
        def _(i):
            for out, first in ((send, 4), (mine, 0)):
                total = dot(held[i, 0, :, :rows], w[first][...])
                total = total + dot(held[i, 0, :, rows:], w[first + 1][...])
                total = total + dot(held[i, 1, :, :rows], w[first + 2][...])
                total = total + dot(held[i, 1, :, rows:], w[first + 3][...])
                out[i] = total.astype(bf16)

    return run(
        kernel,
        [shape((count, tokens, columns), bf16)] * 2,
        8 * count * tokens * half * columns,
        8 * half * columns + 4 * count * tokens * (half + columns),
        index,
        *[a for pair in blocks for a in pair],
        *weights,
        scratch=[pltpu.VMEM((count, 2, tokens, half), bf16)],
    )


def place(index, mine3, mine1, theirs3, theirs1):
    tokens, columns = mine3.shape[1:]

    def kernel(at, a3, a1, b3, b1, out):
        for row, three, one in ((at[4], a3, a1), (1 - at[4], b3, b1)):
            for slot, step in enumerate((0, 1, 3)):
                out[row, at[step]] = three[slot]
            out[row, at[2]] = one[0]

    return run(
        kernel,
        shape((2, NX, tokens, columns), bf16),
        0,
        32 * tokens * columns,
        index,
        mine3,
        mine1,
        theirs3,
        theirs1,
    )


def compute(ssm_output, out_weight, in_weight, gain, residual, proj_cotangent, stream_cotangent):
    depth_scale = 1.0 / math.sqrt(2.0 * LAYERS)
    d = lax.axis_index("dp").astype(jnp.int32)
    t = lax.axis_index("tensor").astype(jnp.int32)
    lane_row = t // NX
    x = t % NX
    resid = residual[0, 0]
    cot_stream = stream_cotangent[0, 0]
    ssm = ssm_output[0, 0]
    tokens = ssm.shape[0]
    block = tokens // 8
    index = jnp.stack([x, (x + 1) % NX, (x + 2) % NX, (x + 3) % NX, lane_row, d, 1 - d, 0 * d])

    ssm = ssm.reshape(2, NX, block, -1)
    cot = proj_cotangent[0, 0].reshape(2, NX, block, -1)
    w_out, w_in = out_weight[0], in_weight[0]
    own = load(lambda at, refs: [refs[0].at[0], refs[0].at[1]], [ssm.shape[1:]] * 2, index, [ssm])
    other = [move(own[0], REPLICA), move(own[1], REPLICA)]
    resid_in = ahead(resid, STAY)
    order = []

    def product(part, rows, steps, adds):
        at = after(index, *order[-1:])
        a, b = row_products(part, rows, steps, at, w_out, adds, steps == (0, 0))
        order.append(a)
        return a, b

    def reduce_start(part):
        far_r, far_l = product(part, (0, 1), (2, 2), ((), ()))
        far_r, far_l = move(far_r, RIGHT), move(far_l, LEFT)
        l0, r1 = product(part, (0, 1), (3, 1), ((), ()))
        return far_r, far_l, move(l0, LEFT), move(r1, RIGHT)

    def reduce_relay(part, started):
        far_r, far_l, l0, r1 = started
        r0, l1 = product(part, (0, 1), (1, 3), ((far_r,), (far_l,)))
        r0, l1 = move(r0, RIGHT), move(l1, LEFT)
        return (l0, r0), (r1, l1)

    def reduce_end(part, arrived):
        return product(part, (0, 1), (0, 0), arrived)

    started = reduce_start(own)
    rows = w_in.shape[0] // 2
    w_a, w_b, cot, cot_send = load(
        lambda at, refs: [
            refs[0].at[pl.ds(0, rows)],
            refs[0].at[pl.ds(rows, rows)],
            refs[1],
            refs[1].at[1 - at[4]],
        ],
        [(rows, w_in.shape[1])] * 2 + [cot.shape, cot.shape[1:]],
        after(index, order[-1]),
        [w_in, cot],
    )
    cot_pair = move(cot_send, PAIR)
    own_arrived = reduce_relay(own, started)
    far_r, l0 = product(other, (0, 0), (2, 3), ((), ()))
    far_r, l0 = move(far_r, RIGHT), move(l0, LEFT)
    far_l, r1 = product(other, (1, 1), (2, 1), ((), ()))
    far_l, r1 = move(far_l, LEFT), move(r1, RIGHT)
    started = far_r, far_l, l0, r1
    keep, pass_on = reduce_end(own, own_arrived)
    keep = ahead(keep, STAY)
    pass_on = ahead(pass_on, PAIR)
    oth_arrived = reduce_relay(other, started)
    to_pair, crossing = reduce_end(other, oth_arrived)
    to_pair = move(to_pair, PAIR)
    crossing = add_terms(index, (crossing, to_pair), bf16)
    crossing = ahead(crossing, CROSS)

    pair_a, cross_b = move(after(w_a, other[1]), PAIR), move(w_b, CROSS)
    pair_b, cross_a = move(w_b, PAIR), move(w_a, CROSS)
    opp_a, opp_b = move(pair_a, CROSS), move(cross_b, PAIR)

    half_d = ((w_a, w_b), (pair_a, pair_b))
    half_o = ((opp_a, opp_b), (cross_a, cross_b))

    def back(jobs):
        return back_products(index, cot, cot_pair, jobs)

    far_r, l0 = back([(2, *half_d, (), bf16), (3, *half_d, (), bf16)])
    far_r, l0 = move(far_r, RIGHT), move(l0, LEFT)
    far_l, r1 = back([(2, *half_o, (), bf16), (1, *half_o, (), bf16)])
    far_l, r1 = move(far_l, LEFT), move(r1, RIGHT)
    r0, l1 = back([(1, *half_d, (far_r,), bf16), (3, *half_o, (far_l,), bf16)])
    r0, l1 = move(r0, RIGHT), move(l1, LEFT)
    grad_d, grad_o = back([(0, *half_d, (), f32), (0, *half_o, (), f32)])

    stream, norm_d, norm_o, inv_rms = stream_and_norm(
        index, resid_in, keep, pass_on, crossing, gain, depth_scale
    )

    d_l, o_r = move(norm_d, RIGHT), move(norm_o, LEFT)
    d_r, o_l = move(norm_d, LEFT), move(norm_o, RIGHT)
    d_f, o_f = move(d_l, RIGHT), move(o_r, LEFT)
    stream_grad, gain_part = norm_backward(
        index, stream, inv_rms, cot_stream, gain, (grad_d, l0, r0), (grad_o, r1, l1)
    )
    resid_grad = store(ahead(stream_grad, STAY, -1))
    for routes in ((ACROSS, RIGHT, LEFT), (REPLICA, PAIR, CROSS)):
        a, b, c = (move(gain_part, r) for r in routes)
        gain_part = add_terms(index, (gain_part, a, b, c), f32)

    weights = (w_a, w_b, opp_a, opp_b, pair_a, pair_b, cross_a, cross_b)
    mine3, send3 = project(index, [(norm_d, norm_o), (d_r, o_r), (d_l, o_l)], weights)
    theirs3 = move(send3, PAIR)
    mine1, send1 = project(index, [(d_f, o_f)], weights)
    theirs1 = move(send1, PAIR)
    projected = place(after(index, resid_grad, gain_part), mine3, mine1, theirs3, theirs1)
    projected = projected.reshape(tokens, -1)

    return stream[None, None], projected[None, None], resid_grad[None, None], gain_part


def solution(mesh):
    in_specs = (
        P("pipe", "dp", None, "tensor"),
        P("pipe", "tensor", "dp"),
        P("pipe", "dp", "tensor"),
        P("pipe", None),
        P("pipe", "dp", "tensor", None),
        P("pipe", "dp", None, "tensor"),
        P("pipe", "dp", "tensor", None),
    )
    out_specs = (
        P("pipe", "dp", "tensor", None),
        P("pipe", "dp", None, "tensor"),
        P("pipe", "dp", "tensor", None),
        P("pipe", None),
    )
    return jax.shard_map(compute, mesh=mesh, in_specs=in_specs, out_specs=out_specs, check_vma=False)
```

time: 477 us -> 213 us (0.45)
  waiting for transfers between devices: 330 us -> 88.4 us
  blocking collectives: 62.7 us -> 0 us
  starting transfers between devices: 2.92 us -> 65 us
  Pallas kernels: 0 us -> 51.6 us
  matrix products: 29.1 us -> 0 us
  local copies, waits for them, and re-layouts: 32.7 us -> 3.91 us
  between operations: 13.9 us -> 1.08 us
  other arithmetic: 5.19 us -> 0 us
    unnamed x7 -> x0, waiting for transfers between devices: 172 us -> none
    all_gather x3 -> x0, waiting for transfers between devices: 158 us -> none  [the longest x1 112 us: body(): lax.all_gather(out_weight, 'dp', axis=2, tiled=True)]
    ppermute x2 -> x47, waiting for transfers between devices: 0.01 us -> 88.4 us  [the longest x42 85.6 us: move(): return lax.ppermute(block, PLANE, route)]
    psum x1 -> x0, blocking collectives: 62.7 us -> none  [body(): gain_total = lax.psum(gain_part, ('dp', 'tensor'))]
    ppermute x2 -> x47, starting transfers between devices: 2.73 us -> 65 us  [the longest x42 62 us: move(): return lax.ppermute(block, PLANE, route)]
    pallas_call x0 -> x23, Pallas kernels: none -> 51.6 us  [the longest x20 49.2 us: run(): pl.pallas_call(kernel, out_shape=out_shape, in_specs=[SMEM] + [VMEM] * le...]
    dot_general x3 -> x0, matrix products: 29.1 us -> none  [the longest x1 14.6 us: body(): jnp.einsum('mtc,cd->tmd', block, w_out, preferred_element_type=jnp.float32)]
    unnamed x18, local copies, waits for them, and re-layouts: 32.7 us -> 3.82 us
  transfers between devices with their start and end apart: 7 -> 47, of which waited for: 5 -> 23; matrix products, arithmetic and copies ran while one was open for 11% -> 0% of each run, Pallas kernels for 0% -> 24%
where the time goes in v1:
time: 213 us; the launch traced here: 210 us
  waiting for transfers between devices  88.4 us (42%)
  starting transfers between devices  65 us (31%)
  Pallas kernels  51.6 us (24%)
  local copies, waits for them, and re-layouts  3.91 us (2%)
    ppermute x42, waiting for transfers between devices, move(): return lax.ppermute(block, PLANE, route)  85.6 us
    ppermute x42, starting transfers between devices, move(): return lax.ppermute(block, PLANE, route)  62 us
    pallas_call x20, Pallas kernels, run(): pl.pallas_call(kernel, out_shape=out_shape, in_specs=[SMEM] + [VMEM] * le...  49.2 us
  transfers between devices with their start and end apart: 47, of which 23 were waited for; matrix products, arithmetic and copies ran while one was open for 0% of the time, Pallas kernels for 24%

profile of v1, /device:TPU:16, one launch (start us, length us, event | category | flops | bytes accessed | tf_op | source)
XLA Modules:
  0.0 210.0 jit_solution(7631939328624284896)
XLA Ops:
  17.3 7.4 %collective-permute-done.2.rest_1_ = bf16[128,2048]{1,0:T(8,128)(2,1)S(1)} collective-permute-done((bf16[128,2048]{1,0:T(8,128)(2,1)S(1)}, bf16[128,2048]{1,0:T(8,128)(2,1)S(1)}, u32[]{:S(2)}, u32[]{:S(2)}) %collective-permute-start.2) | collective-permute-done | bytes 524320 | tf_op jit(solution)/shard_map/ppermute | solution.py:41
  24.7 3.7 %collective-permute-start.5 = (bf16[128,2048]{1,0:T(8,128)(2,1)S(1)}, bf16[128,2048]{1,0:T(8,128)(2,1)S(1)}, u32[]{:S(2)}, u32[]{:S(2)}) collective-permute-start(bf16[128,2048]{1,0:T(8,128)(2,1)S(1)} %get-tuple-element.57), channel_id=1, source_target_pairs={{0,3},{1,0},{2,1},{3,2},{4,7},{5,4},{6,5},{7,6},{8,11},{9,8},{10,9... | collective-permute-start | bytes 1572872 | tf_op jit(solution)/shard_map/ppermute | solution.py:41
  37.0 15.1 %collective-permute-done.4.one_ref.two_ref = bf16[4,128,1024]{2,1,0:T(8,128)(2,1)S(1)} collective-permute-done((bf16[4,128,1024]{2,1,0:T(8,128)(2,1)S(1)}, bf16[4,128,1024]{2,1,0:T(8,128)(2,1)S(1)}, u32[]{:S(2)}, u32[]{:S(2)}) %collective-permute-start.4) | collective-permute-done | bytes 1048608 | tf_op jit(solution)/shard_map/ppermute | solution.py:41
  66.3 4.4 %collective-permute-done.12.rest_1_ = bf16[128,2048]{1,0:T(8,128)(2,1)S(1)} collective-permute-done((bf16[128,2048]{1,0:T(8,128)(2,1)S(1)}, bf16[128,2048]{1,0:T(8,128)(2,1)S(1)}, u32[]{:S(2)}, u32[]{:S(2)}) %collective-permute-start.12) | collective-permute-done | bytes 524320 | tf_op jit(solution)/shard_map/ppermute | solution.py:41
  74.4 3.0 %collective-permute-start.16 = (bf16[128,2048]{1,0:T(8,128)(2,1)S(1)}, bf16[128,2048]{1,0:T(8,128)(2,1)S(1)}, u32[]{:S(2)}, u32[]{:S(2)}) collective-permute-start(bf16[128,2048]{1,0:T(8,128)(2,1)S(1)} %get-tuple-element.75), channel_id=1, source_target_pairs={{0,3},{1,0},{2,1},{3,2},{4,7},{5,4},{6,5},{7,6},{8,11},{9,8},{10,9... | collective-permute-start | bytes 1572872 | tf_op jit(solution)/shard_map/ppermute | solution.py:41
  77.5 4.5 %collective-permute-done.13.rest_0_ = bf16[128,2048]{1,0:T(8,128)(2,1)S(1)} collective-permute-done((bf16[128,2048]{1,0:T(8,128)(2,1)S(1)}, bf16[128,2048]{1,0:T(8,128)(2,1)S(1)}, u32[]{:S(2)}, u32[]{:S(2)}) %collective-permute-start.13) | collective-permute-done | bytes 524320 | tf_op jit(solution)/shard_map/ppermute | solution.py:41
  85.1 5.9 %collective-permute-done.16.rest_3_ = bf16[128,2048]{1,0:T(8,128)(2,1)S(1)} collective-permute-done((bf16[128,2048]{1,0:T(8,128)(2,1)S(1)}, bf16[128,2048]{1,0:T(8,128)(2,1)S(1)}, u32[]{:S(2)}, u32[]{:S(2)}) %collective-permute-start.16) | collective-permute-done | bytes 524320 | tf_op jit(solution)/shard_map/ppermute | solution.py:41
  98.1 4.2 %shard_map.115 = (bf16[128,2048]{1,0:T(8,128)(2,1)S(1)}, bf16[128,2048]{1,0:T(8,128)(2,1)S(1)}) custom-call(s32[8]{0:T(128)S(1)} %stack.31.at, bf16[2,4,128,256]{3,2,1,0:T(8,128)(2,1)S(1)} %get-tuple-element.80.cot_ref, bf16[4,128,256]{2,1,0:T(8,128)(2,1)S(1)} %collective-permute-done.19.pair_ref, ...), custom_call_target="tpu_custom_call" | custom-call | flops 536870912 | bytes 4194304 | tf_op jit(solution)/shard_map/pallas_call | solution.py:73
  106.7 4.2 %shard_map.116 = (bf16[128,2048]{1,0:T(8,128)(2,1)S(1)}, bf16[128,2048]{1,0:T(8,128)(2,1)S(1)}) custom-call(s32[8]{0:T(128)S(1)} %stack.31.at, bf16[2,4,128,256]{3,2,1,0:T(8,128)(2,1)S(1)} %get-tuple-element.80.cot_ref, bf16[4,128,256]{2,1,0:T(8,128)(2,1)S(1)} %collective-permute-done.19.pair_ref, ...), custom_call_target="tpu_custom_call" | custom-call | flops 536870912 | bytes 4194304 | tf_op jit(solution)/shard_map/pallas_call | solution.py:73
  110.9 3.0 %collective-permute-start.28 = (bf16[128,2048]{1,0:T(8,128)(2,1)S(1)}, bf16[128,2048]{1,0:T(8,128)(2,1)S(1)}, u32[]{:S(2)}, u32[]{:S(2)}) collective-permute-start(bf16[128,2048]{1,0:T(8,128)(2,1)S(1)} %get-tuple-element.88), channel_id=1, source_target_pairs={{0,3},{1,0},{2,1},{3,2},{4,7},{5,4},{6,5},{7,6},{8,11},{9,8},{10,9... | collective-permute-start | bytes 1572872 | tf_op jit(solution)/shard_map/ppermute | solution.py:41
  117.6 3.0 %collective-permute-done.28.refs_9_ = bf16[128,2048]{1,0:T(8,128)(2,1)S(1)} collective-permute-done((bf16[128,2048]{1,0:T(8,128)(2,1)S(1)}, bf16[128,2048]{1,0:T(8,128)(2,1)S(1)}, u32[]{:S(2)}, u32[]{:S(2)}) %collective-permute-start.28) | collective-permute-done | bytes 524320 | tf_op jit(solution)/shard_map/ppermute | solution.py:41
  120.5 3.7 %collective-permute-start.26 = (bf16[128,2048]{1,0:T(8,128)(2,1)S(1)}, bf16[128,2048]{1,0:T(8,128)(2,1)S(1)}, u32[]{:S(2)}, u32[]{:S(2)}) collective-permute-start(bf16[128,2048]{1,0:T(8,128)(2,1)S(1)} %get-tuple-element.86), channel_id=1, source_target_pairs={{0,3},{1,0},{2,1},{3,2},{4,7},{5,4},{6,5},{7,6},{8,11},{9,8},{10,9... | collective-permute-start | bytes 1572872 | tf_op jit(solution)/shard_map/ppermute | solution.py:41
  124.2 4.2 %shard_map.117 = (bf16[128,2048]{1,0:T(8,128)(2,1)S(1)}, bf16[128,2048]{1,0:T(8,128)(2,1)S(1)}) custom-call(s32[8]{0:T(128)S(1)} %stack.31.at, bf16[2,4,128,256]{3,2,1,0:T(8,128)(2,1)S(1)} %get-tuple-element.80.cot_ref, bf16[4,128,256]{2,1,0:T(8,128)(2,1)S(1)} %collective-permute-done.19.pair_ref, ...), custom_call_target="tpu_custom_call" | custom-call | flops 536870912 | bytes 10485760 | tf_op jit(solution)/shard_map/pallas_call | solution.py:73
  136.2 3.2 %collective-permute-start.40 = (bf16[128,2048]{1,0:T(8,128)(2,1)S(1)}, bf16[128,2048]{1,0:T(8,128)(2,1)S(1)}, u32[]{:S(2)}, u32[]{:S(2)}) collective-permute-start(bf16[128,2048]{1,0:T(8,128)(2,1)S(1)} %get-tuple-element.97.refs_1_), channel_id=1, source_target_pairs={{0,3},{1,0},{2,1},{3,2},{4,7},{5,4},{6,5},{7,6},{8,11},{9,8},{10,9... | collective-permute-start | bytes 1572872 | tf_op jit(solution)/shard_map/ppermute | solution.py:41
  139.4 4.2 %shard_map.114 = (f32[128,2048]{1,0:T(8,128)S(1)}, f32[128,2048]{1,0:T(8,128)S(1)}) custom-call(s32[8]{0:T(128)S(1)} %stack.31.at, bf16[2,4,128,256]{3,2,1,0:T(8,128)(2,1)S(1)} %get-tuple-element.80.cot_ref, bf16[4,128,256]{2,1,0:T(8,128)(2,1)S(1)} %collective-permute-done.19.pair_ref, bf16[1024,256]{1,0:T(8,128)(2,1)S(1)} %get-tuple-element.84.refs_0_.refs_6_.refs_2_, ...), custom_call_target="tpu_custom_call" | custom-call | flops 536870912 | bytes 8388608 | tf_op jit(solution)/shard_map/pallas_call | solution.py:73
  144.5 11.2 %collective-permute-done.29.h2 = bf16[128,2048]{1,0:T(8,128)(2,1)S(1)} collective-permute-done((bf16[128,2048]{1,0:T(8,128)(2,1)S(1)}, bf16[128,2048]{1,0:T(8,128)(2,1)S(1)}, u32[]{:S(2)}, u32[]{:S(2)}) %collective-permute-start.29) | collective-permute-done | bytes 524320 | tf_op jit(solution)/shard_map/ppermute | solution.py:41
  162.2 3.2 %collective-permute-start.44 = (bf16[128,2048]{1,0:T(8,128)(2,1)S(1)}, bf16[128,2048]{1,0:T(8,128)(2,1)S(1)}, u32[]{:S(2)}, u32[]{:S(2)}) collective-permute-start(bf16[128,2048]{1,0:T(8,128)(2,1)S(1)} %collective-permute-done.40.refs_3_), channel_id=1, source_target_pairs={{0,3},{1,0},{2,1},{3,2},{4,7},{5,4},{6,5},{7,6},{8,11},{9,8},{10,9... | collective-permute-start | bytes 1572872 | tf_op jit(solution)/shard_map/ppermute | solution.py:41
  165.4 7.7 %collective-permute-done.39.refs_2_ = bf16[128,2048]{1,0:T(8,128)(2,1)S(1)} collective-permute-done((bf16[128,2048]{1,0:T(8,128)(2,1)S(1)}, bf16[128,2048]{1,0:T(8,128)(2,1)S(1)}, u32[]{:S(2)}, u32[]{:S(2)}) %collective-permute-start.39) | collective-permute-done | bytes 524320 | tf_op jit(solution)/shard_map/ppermute | solution.py:41
  174.4 3.0 %shard_map.121 = (bf16[3,128,256]{2,1,0:T(8,128)(2,1)S(1)}, bf16[3,128,256]{2,1,0:T(8,128)(2,1)S(1)}) custom-call(s32[8]{0:T(128)S(1)} %stack.31.at, bf16[128,2048]{1,0:T(8,128)(2,1)S(1)} %get-tuple-element.96.refs_0_, bf16[128,2048]{1,0:T(8,128)(2,1)S(1)} %get-tuple-element.97.refs_1_, bf16[128,2048]{1,0:T(8,128)(2,1)S(1)} %collective-permute-done.39.refs_2_, ...), custom_call_target="tpu_custom_call" | custom-call | flops 1610612736 | bytes 7733248 | tf_op jit(solution)/shard_map/pallas_call | solution.py:73
  177.4 6.1 %collective-permute-start.45 = (bf16[3,128,256]{2,1,0:T(8,128)(2,1)S(1)}, bf16[3,128,256]{2,1,0:T(8,128)(2,1)S(1)}, u32[]{:S(2)}, u32[]{:S(2)}) collective-permute-start(bf16[3,128,256]{2,1,0:T(8,128)(2,1)S(1)} %get-tuple-element.100), channel_id=1, source_target_pairs={{0,4},{1,5},{2,6},{3,7},{4,0},{5,1},{6,2},{7,3},{8,12},{9,13},{10,... | collective-permute-start | bytes 589832 | tf_op jit(solution)/shard_map/ppermute | solution.py:41
  186.3 5.3 %collective-permute-start.46 = (bf16[1,128,256]{2,1,0:T(8,128)(2,1)S(1)}, bf16[1,128,256]{2,1,0:T(8,128)(2,1)S(1)}, u32[]{:S(2)}, u32[]{:S(2)}) collective-permute-start(bf16[1,128,256]{2,1,0:T(8,128)(2,1)S(1)} %get-tuple-element.101), channel_id=1, source_target_pairs={{0,4},{1,5},{2,6},{3,7},{4,0},{5,1},{6,2},{7,3},{8,12},{9,13},{10,... | collective-permute-start | bytes 196616 | tf_op jit(solution)/shard_map/ppermute | solution.py:41
  192.6 3.9 %collective-permute-done.34.refs_2_ = f32[1,4096]{1,0:T(1,128)S(1)} collective-permute-done((f32[1,4096]{1,0:T(1,128)S(1)}, f32[1,4096]{1,0:T(1,128)S(1)}, u32[]{:S(2)}, u32[]{:S(2)}) %collective-permute-start.34) | collective-permute-done | bytes 16416 | tf_op jit(solution)/shard_map/ppermute | solution.py:41
  198.3 2.9 %collective-permute-done.38.refs_3_ = f32[1,4096]{1,0:T(1,128)S(1)} collective-permute-done((f32[1,4096]{1,0:T(1,128)S(1)}, f32[1,4096]{1,0:T(1,128)S(1)}, u32[]{:S(2)}, u32[]{:S(2)}) %collective-permute-start.38) | collective-permute-done | bytes 16416 | tf_op jit(solution)/shard_map/ppermute | solution.py:41
  202.1 4.4 %collective-permute-done.36.refs_1_ = f32[1,4096]{1,0:T(1,128)S(1)} collective-permute-done((f32[1,4096]{1,0:T(1,128)S(1)}, f32[1,4096]{1,0:T(1,128)S(1)}, u32[]{:S(2)}, u32[]{:S(2)}) %collective-permute-start.36) | collective-permute-done | bytes 16416 | tf_op jit(solution)/shard_map/ppermute | solution.py:41
  (112 shorter events, 87.5 us)
Async XLA Ops:
  3.1 29.5 %collective-permute-start.3 = (bf16[4,128,1024]{2,1,0:T(8,128)(2,1)S(1)}, bf16[4,128,1024]{2,1,0:T(8,128)(2,1)S(1)}, u32[]{:S(2)}, u32[]{:S(2)}) collective-permute-start(bf16[4,128,1024]{2,1,0:T(8,128)(2,1)S(1)} %get-tuple-element.53.one_ref), channel_id=1, source_target_pairs={{0,8},{1,9},{2,10},{3,11},{4,12},{5,13},{6,14},{7,15},{8,0},{9,1},... | collective-permute-start | bytes 3145736 | tf_op jit(solution)/shard_map/ppermute | solution.py:41
  5.2 46.8 %collective-permute-start.4 = (bf16[4,128,1024]{2,1,0:T(8,128)(2,1)S(1)}, bf16[4,128,1024]{2,1,0:T(8,128)(2,1)S(1)}, u32[]{:S(2)}, u32[]{:S(2)}) collective-permute-start(bf16[4,128,1024]{2,1,0:T(8,128)(2,1)S(1)} %get-tuple-element.54.two_ref), channel_id=1, source_target_pairs={{0,8},{1,9},{2,10},{3,11},{4,12},{5,13},{6,14},{7,15},{8,0},{9,1},... | collective-permute-start | bytes 3145736 | tf_op jit(solution)/shard_map/ppermute | solution.py:41
  16.5 39.4 %collective-permute-start.7 = (bf16[128,2048]{1,0:T(8,128)(2,1)S(1)}, bf16[128,2048]{1,0:T(8,128)(2,1)S(1)}, u32[]{:S(2)}, u32[]{:S(2)}) collective-permute-start(bf16[128,2048]{1,0:T(8,128)(2,1)S(1)} %get-tuple-element.66), channel_id=1, source_target_pairs={{0,1},{1,2},{2,3},{3,0},{4,5},{5,6},{6,7},{7,4},{8,9},{9,10},{10,1... | collective-permute-start | bytes 1572872 | tf_op jit(solution)/shard_map/ppermute | solution.py:41
  24.7 33.7 %collective-permute-start.5 = (bf16[128,2048]{1,0:T(8,128)(2,1)S(1)}, bf16[128,2048]{1,0:T(8,128)(2,1)S(1)}, u32[]{:S(2)}, u32[]{:S(2)}) collective-permute-start(bf16[128,2048]{1,0:T(8,128)(2,1)S(1)} %get-tuple-element.57), channel_id=1, source_target_pairs={{0,3},{1,0},{2,1},{3,2},{4,7},{5,4},{6,5},{7,6},{8,11},{9,8},{10,9... | collective-permute-start | bytes 1572872 | tf_op jit(solution)/shard_map/ppermute | solution.py:41
  32.5 26.5 %collective-permute-start.8 = (bf16[128,2048]{1,0:T(8,128)(2,1)S(1)}, bf16[128,2048]{1,0:T(8,128)(2,1)S(1)}, u32[]{:S(2)}, u32[]{:S(2)}) collective-permute-start(bf16[128,2048]{1,0:T(8,128)(2,1)S(1)} %get-tuple-element.67), channel_id=1, source_target_pairs={{0,3},{1,0},{2,1},{3,2},{4,7},{5,4},{6,5},{7,6},{8,11},{9,8},{10,9... | collective-permute-start | bytes 1572872 | tf_op jit(solution)/shard_map/ppermute | solution.py:41
  32.6 28.0 %collective-permute-start.6 = (bf16[128,2048]{1,0:T(8,128)(2,1)S(1)}, bf16[128,2048]{1,0:T(8,128)(2,1)S(1)}, u32[]{:S(2)}, u32[]{:S(2)}) collective-permute-start(bf16[128,2048]{1,0:T(8,128)(2,1)S(1)} %get-tuple-element.60), channel_id=1, source_target_pairs={{0,1},{1,2},{2,3},{3,0},{4,5},{5,6},{6,7},{7,4},{8,9},{9,10},{10,1... | collective-permute-start | bytes 1572872 | tf_op jit(solution)/shard_map/ppermute | solution.py:41
  58.5 19.0 %collective-permute-start.23 = (bf16[1024,256]{1,0:T(8,128)(2,1)S(1)}, bf16[1024,256]{1,0:T(8,128)(2,1)S(1)}, u32[]{:S(2)}, u32[]{:S(2)}) collective-permute-start(bf16[1024,256]{1,0:T(8,128)(2,1)S(1)} %get-tuple-element.83.refs_1_.refs_7_.refs_3_), channel_id=1, source_target_pairs={{0,12},{1,13},{2,14},{3,15},{4,8},{5,9},{6,10},{7,11},{8,4},{9,5},... | collective-permute-start | bytes 1572872 | tf_op jit(solution)/shard_map/ppermute | solution.py:41
  59.0 23.0 %collective-permute-start.13 = (bf16[128,2048]{1,0:T(8,128)(2,1)S(1)}, bf16[128,2048]{1,0:T(8,128)(2,1)S(1)}, u32[]{:S(2)}, u32[]{:S(2)}) collective-permute-start(bf16[128,2048]{1,0:T(8,128)(2,1)S(1)} %get-tuple-element.73), channel_id=1, source_target_pairs={{0,3},{1,0},{2,1},{3,2},{4,7},{5,4},{6,5},{7,6},{8,11},{9,8},{10,9... | collective-permute-start | bytes 1572872 | tf_op jit(solution)/shard_map/ppermute | solution.py:41
  66.1 17.2 %collective-permute-start.15 = (bf16[128,2048]{1,0:T(8,128)(2,1)S(1)}, bf16[128,2048]{1,0:T(8,128)(2,1)S(1)}, u32[]{:S(2)}, u32[]{:S(2)}) collective-permute-start(bf16[128,2048]{1,0:T(8,128)(2,1)S(1)} %get-tuple-element.74), channel_id=1, source_target_pairs={{0,1},{1,2},{2,3},{3,0},{4,5},{5,6},{6,7},{7,4},{8,9},{9,10},{10,1... | collective-permute-start | bytes 1572872 | tf_op jit(solution)/shard_map/ppermute | solution.py:41
  74.4 16.6 %collective-permute-start.16 = (bf16[128,2048]{1,0:T(8,128)(2,1)S(1)}, bf16[128,2048]{1,0:T(8,128)(2,1)S(1)}, u32[]{:S(2)}, u32[]{:S(2)}) collective-permute-start(bf16[128,2048]{1,0:T(8,128)(2,1)S(1)} %get-tuple-element.75), channel_id=1, source_target_pairs={{0,3},{1,0},{2,1},{3,2},{4,7},{5,4},{6,5},{7,6},{8,11},{9,8},{10,9... | collective-permute-start | bytes 1572872 | tf_op jit(solution)/shard_map/ppermute | solution.py:41
  83.3 19.0 %collective-permute-start.25 = (bf16[1024,256]{1,0:T(8,128)(2,1)S(1)}, bf16[1024,256]{1,0:T(8,128)(2,1)S(1)}, u32[]{:S(2)}, u32[]{:S(2)}) collective-permute-start(bf16[1024,256]{1,0:T(8,128)(2,1)S(1)} %get-tuple-element.84.refs_0_.refs_6_.refs_2_), channel_id=1, source_target_pairs={{0,12},{1,13},{2,14},{3,15},{4,8},{5,9},{6,10},{7,11},{8,4},{9,5},... | collective-permute-start | bytes 1572872 | tf_op jit(solution)/shard_map/ppermute | solution.py:41
  83.3 23.3 %collective-permute-start.24 = (bf16[1024,256]{1,0:T(8,128)(2,1)S(1)}, bf16[1024,256]{1,0:T(8,128)(2,1)S(1)}, u32[]{:S(2)}, u32[]{:S(2)}) collective-permute-start(bf16[1024,256]{1,0:T(8,128)(2,1)S(1)} %collective-permute-done.23.refs_7_.refs_3_.refs_8_.refs_13_.refs_9_), channel_id=1, source_target_pairs={{0,4},{1,5},{2,6},{3,7},{4,0},{5,1},{6,2},{7,3},{8,12},{9,13},{10,... | collective-permute-start | bytes 1572872 | tf_op jit(solution)/shard_map/ppermute | solution.py:41
  91.4 37.0 %collective-permute-start = (bf16[128,4096]{1,0:T(8,128)(2,1)S(1)}, bf16[128,4096]{1,0:T(8,128)(2,1)S(1)}, u32[]{:S(2)}, u32[]{:S(2)}) collective-permute-start(bf16[128,4096]{1,0:T(8,128)(2,1)S(1)} %bitcast.31), channel_id=1, source_target_pairs={{0,16},{1,17},{2,18},{3,19},{4,20},{5,21},{6,22},{7,23},{8,24},{9,... | collective-permute-start | bytes 3145736 | tf_op jit(solution)/shard_map/ppermute | solution.py:52
  96.8 17.1 %collective-permute-start.17 = (bf16[128,2048]{1,0:T(8,128)(2,1)S(1)}, bf16[128,2048]{1,0:T(8,128)(2,1)S(1)}, u32[]{:S(2)}, u32[]{:S(2)}) collective-permute-start(bf16[128,2048]{1,0:T(8,128)(2,1)S(1)} %get-tuple-element.77), channel_id=1, source_target_pairs={{0,4},{1,5},{2,6},{3,7},{4,0},{5,1},{6,2},{7,3},{8,12},{9,13},{10,... | collective-permute-start | bytes 1572872 | tf_op jit(solution)/shard_map/ppermute | solution.py:41
  113.9 16.3 %collective-permute-start.9 = (bf16[128,2048]{1,0:T(8,128)(2,1)S(1)}, bf16[128,2048]{1,0:T(8,128)(2,1)S(1)}, u32[]{:S(2)}, u32[]{:S(2)}) collective-permute-start(bf16[128,2048]{1,0:T(8,128)(2,1)S(1)} %get-tuple-element.68), channel_id=1, source_target_pairs={{0,16},{1,17},{2,18},{3,19},{4,20},{5,21},{6,22},{7,23},{8,24},{9,... | collective-permute-start | bytes 1572872 | tf_op jit(solution)/shard_map/ppermute | solution.py:52
  128.6 27.2 %collective-permute-start.29 = (bf16[128,2048]{1,0:T(8,128)(2,1)S(1)}, bf16[128,2048]{1,0:T(8,128)(2,1)S(1)}, u32[]{:S(2)}, u32[]{:S(2)}) collective-permute-start(bf16[128,2048]{1,0:T(8,128)(2,1)S(1)} %get-tuple-element.89), channel_id=1, source_target_pairs={{0,1},{1,2},{2,3},{3,0},{4,5},{5,6},{6,7},{7,4},{8,9},{9,10},{10,1... | collective-permute-start | bytes 1572872 | tf_op jit(solution)/shard_map/ppermute | solution.py:41
  130.2 25.6 %collective-permute-start.31 = (bf16[128,2048]{1,0:T(8,128)(2,1)S(1)}, bf16[128,2048]{1,0:T(8,128)(2,1)S(1)}, u32[]{:S(2)}, u32[]{:S(2)}) collective-permute-start(bf16[128,2048]{1,0:T(8,128)(2,1)S(1)} %get-tuple-element.92), channel_id=1, source_target_pairs={{0,3},{1,0},{2,1},{3,2},{4,7},{5,4},{6,5},{7,6},{8,11},{9,8},{10,9... | collective-permute-start | bytes 1572872 | tf_op jit(solution)/shard_map/ppermute | solution.py:41
  136.2 26.0 %collective-permute-start.41 = (bf16[128,2048]{1,0:T(8,128)(2,1)S(1)}, bf16[128,2048]{1,0:T(8,128)(2,1)S(1)}, u32[]{:S(2)}, u32[]{:S(2)}) collective-permute-start(bf16[128,2048]{1,0:T(8,128)(2,1)S(1)} %get-tuple-element.96.refs_0_), channel_id=1, source_target_pairs={{0,1},{1,2},{2,3},{3,0},{4,5},{5,6},{6,7},{7,4},{8,9},{9,10},{10,1... | collective-permute-start | bytes 1572872 | tf_op jit(solution)/shard_map/ppermute | solution.py:41
  136.2 26.0 %collective-permute-start.40 = (bf16[128,2048]{1,0:T(8,128)(2,1)S(1)}, bf16[128,2048]{1,0:T(8,128)(2,1)S(1)}, u32[]{:S(2)}, u32[]{:S(2)}) collective-permute-start(bf16[128,2048]{1,0:T(8,128)(2,1)S(1)} %get-tuple-element.97.refs_1_), channel_id=1, source_target_pairs={{0,3},{1,0},{2,1},{3,2},{4,7},{5,4},{6,5},{7,6},{8,11},{9,8},{10,9... | collective-permute-start | bytes 1572872 | tf_op jit(solution)/shard_map/ppermute | solution.py:41
  158.2 49.4 %collective-permute-start.32 = (bf16[128,4096]{1,0:T(8,128)(2,1)S(1)}, bf16[128,4096]{1,0:T(8,128)(2,1)S(1)}, u32[]{:S(2)}, u32[]{:S(2)}) collective-permute-start(bf16[128,4096]{1,0:T(8,128)(2,1)S(1)} %get-tuple-element.93), channel_id=1, source_target_pairs={{0,240},{1,241},{2,242},{3,243},{4,244},{5,245},{6,246},{7,247},{8... | collective-permute-start | bytes 3145736 | tf_op jit(solution)/shard_map/ppermute | solution.py:52
  162.2 22.9 %collective-permute-start.43 = (bf16[128,2048]{1,0:T(8,128)(2,1)S(1)}, bf16[128,2048]{1,0:T(8,128)(2,1)S(1)}, u32[]{:S(2)}, u32[]{:S(2)}) collective-permute-start(bf16[128,2048]{1,0:T(8,128)(2,1)S(1)} %collective-permute-done.41.refs_4_), channel_id=1, source_target_pairs={{0,1},{1,2},{2,3},{3,0},{4,5},{5,6},{6,7},{7,4},{8,9},{9,10},{10,1... | collective-permute-start | bytes 1572872 | tf_op jit(solution)/shard_map/ppermute | solution.py:41
  162.2 22.9 %collective-permute-start.44 = (bf16[128,2048]{1,0:T(8,128)(2,1)S(1)}, bf16[128,2048]{1,0:T(8,128)(2,1)S(1)}, u32[]{:S(2)}, u32[]{:S(2)}) collective-permute-start(bf16[128,2048]{1,0:T(8,128)(2,1)S(1)} %collective-permute-done.40.refs_3_), channel_id=1, source_target_pairs={{0,3},{1,0},{2,1},{3,2},{4,7},{5,4},{6,5},{7,6},{8,11},{9,8},{10,9... | collective-permute-start | bytes 1572872 | tf_op jit(solution)/shard_map/ppermute | solution.py:41
  177.4 31.2 %collective-permute-start.45 = (bf16[3,128,256]{2,1,0:T(8,128)(2,1)S(1)}, bf16[3,128,256]{2,1,0:T(8,128)(2,1)S(1)}, u32[]{:S(2)}, u32[]{:S(2)}) collective-permute-start(bf16[3,128,256]{2,1,0:T(8,128)(2,1)S(1)} %get-tuple-element.100), channel_id=1, source_target_pairs={{0,4},{1,5},{2,6},{3,7},{4,0},{5,1},{6,2},{7,3},{8,12},{9,13},{10,... | collective-permute-start | bytes 589832 | tf_op jit(solution)/shard_map/ppermute | solution.py:41
  186.3 22.3 %collective-permute-start.46 = (bf16[1,128,256]{2,1,0:T(8,128)(2,1)S(1)}, bf16[1,128,256]{2,1,0:T(8,128)(2,1)S(1)}, u32[]{:S(2)}, u32[]{:S(2)}) collective-permute-start(bf16[1,128,256]{2,1,0:T(8,128)(2,1)S(1)} %get-tuple-element.101), channel_id=1, source_target_pairs={{0,4},{1,5},{2,6},{3,7},{4,0},{5,1},{6,2},{7,3},{8,12},{9,13},{10,... | collective-permute-start | bytes 196616 | tf_op jit(solution)/shard_map/ppermute | solution.py:41
  (32 other events, 439.5 us)

commit v2 on v1

--- a/solution.py
+++ b/solution.py
@@ -121,10 +121,10 @@
     )
 
 
-def back_products(index, cot, cot_pair, jobs):
+def back_products(index, cot, cot_pair, jobs, deep=256):
     tokens = cot.shape[2]
     rows = jobs[0][1][0].shape[0]
-    deep = min(256, rows)
+    deep = min(deep, rows)
     operands, plan = [], []
     for step, mine, theirs, adds, dtype in jobs:
         spots = []
@@ -135,8 +135,25 @@
             spots.append(known[0] if known else len(operands) - 1)
         plan.append((step, spots, dtype))
 
+    together = len(jobs) == 2 and plan[0][1] == plan[1][1] and len(plan[0][1]) == 4
+
     def kernel(at, cot_ref, pair_ref, *refs):
         outs = refs[len(operands) :]
+        if together:
+            steps, spots = [at[step] for step, _, _ in plan], plan[0][1]
+            a = jnp.concatenate([cot_ref[at[4], step] for step in steps], axis=0)
+            b = jnp.concatenate([pair_ref[step] for step in steps], axis=0)
+            for i in range(2):
+
+                @pl.loop(0, rows // deep)
+                def _(n):
+                    own = pl.ds(pl.multiple_of(n * deep, deep), deep)
+                    cols = pl.ds(pl.multiple_of(i * rows + n * deep, deep), deep)
+                    value = dot_t(a, refs[spots[i]][own]) + dot_t(b, refs[spots[2 + i]][own])
+                    outs[0][:, cols] = value[:tokens].astype(plan[0][2])
+                    outs[1][:, cols] = value[tokens:].astype(plan[1][2])
+
+            return
         for (step, spots, dtype), out in zip(plan, outs):
             a, b = cot_ref[at[4], at[step]], pair_ref[at[step]]
             for i in range(2):
@@ -437,14 +454,14 @@
     half_d = ((w_a, w_b), (pair_a, pair_b))
     half_o = ((opp_a, opp_b), (cross_a, cross_b))
 
-    def back(jobs):
-        return back_products(index, cot, cot_pair, jobs)
+    def back(jobs, deep=256):
+        return back_products(index, cot, cot_pair, jobs, deep)
 
     far_r, l0 = back([(2, *half_d, (), bf16), (3, *half_d, (), bf16)])
     far_r, l0 = move(far_r, RIGHT), move(l0, LEFT)
     far_l, r1 = back([(2, *half_o, (), bf16), (1, *half_o, (), bf16)])
     far_l, r1 = move(far_l, LEFT), move(r1, RIGHT)
-    r0, l1 = back([(1, *half_d, (far_r,), bf16), (3, *half_o, (far_l,), bf16)])
+    r0, l1 = back([(1, *half_d, (far_r,), bf16), (3, *half_o, (far_l,), bf16)], 512)
     r0, l1 = move(r0, RIGHT), move(l1, LEFT)
     grad_d, grad_o = back([(0, *half_d, (), f32), (0, *half_o, (), f32)])
 

time: 213 us -> 212 us (level)
  Pallas kernels: 51.6 us -> 47.4 us
    pallas_call x20, Pallas kernels: 49.2 us -> 45 us  [run(): pl.pallas_call(kernel, out_shape=out_shape, in_specs=[SMEM] + [VMEM] * le...]
    ppermute x42, waiting for transfers between devices: 85.6 us -> 89.6 us  [move(): return lax.ppermute(block, PLANE, route)]
    ppermute x5, waiting for transfers between devices: 2.83 us -> 0.01 us  [ahead(): return lax.ppermute(block, ALL, full)]
    ppermute x42, starting transfers between devices: 62 us -> 64.7 us  [move(): return lax.ppermute(block, PLANE, route)]
  transfers between devices with their start and end apart: 47 -> 47, of which waited for: 23 -> 20; matrix products, arithmetic and copies ran while one was open for 0% -> 0% of each run, Pallas kernels for 24% -> 22%
where the time goes in v2:
time: 212 us; the launch traced here: 209 us
  waiting for transfers between devices  89.6 us (42%)
  starting transfers between devices  66.9 us (32%)
  Pallas kernels  47.4 us (22%)
  local copies, waits for them, and re-layouts  3.91 us (2%)
    ppermute x42, waiting for transfers between devices, move(): return lax.ppermute(block, PLANE, route)  89.6 us
    ppermute x42, starting transfers between devices, move(): return lax.ppermute(block, PLANE, route)  64.7 us
    pallas_call x20, Pallas kernels, run(): pl.pallas_call(kernel, out_shape=out_shape, in_specs=[SMEM] + [VMEM] * le...  45 us
  transfers between devices with their start and end apart: 47, of which 20 were waited for; matrix products, arithmetic and copies ran while one was open for 0% of the time, Pallas kernels for 22%

profile of v2, /device:TPU:16, one launch (start us, length us, event | category | flops | bytes accessed | tf_op | source)
XLA Modules:
  0.0 208.8 jit_solution(8737947602718306011)
XLA Ops:
  17.3 7.4 %collective-permute-done.2.rest_1_ = bf16[128,2048]{1,0:T(8,128)(2,1)S(1)} collective-permute-done((bf16[128,2048]{1,0:T(8,128)(2,1)S(1)}, bf16[128,2048]{1,0:T(8,128)(2,1)S(1)}, u32[]{:S(2)}, u32[]{:S(2)}) %collective-permute-start.2) | collective-permute-done | bytes 524320 | tf_op jit(solution)/shard_map/ppermute | solution.py:41
  24.7 3.7 %collective-permute-start.5 = (bf16[128,2048]{1,0:T(8,128)(2,1)S(1)}, bf16[128,2048]{1,0:T(8,128)(2,1)S(1)}, u32[]{:S(2)}, u32[]{:S(2)}) collective-permute-start(bf16[128,2048]{1,0:T(8,128)(2,1)S(1)} %get-tuple-element.57), channel_id=1, source_target_pairs={{0,3},{1,0},{2,1},{3,2},{4,7},{5,4},{6,5},{7,6},{8,11},{9,8},{10,9... | collective-permute-start | bytes 1572872 | tf_op jit(solution)/shard_map/ppermute | solution.py:41
  37.0 15.1 %collective-permute-done.4.one_ref.two_ref = bf16[4,128,1024]{2,1,0:T(8,128)(2,1)S(1)} collective-permute-done((bf16[4,128,1024]{2,1,0:T(8,128)(2,1)S(1)}, bf16[4,128,1024]{2,1,0:T(8,128)(2,1)S(1)}, u32[]{:S(2)}, u32[]{:S(2)}) %collective-permute-start.4) | collective-permute-done | bytes 1048608 | tf_op jit(solution)/shard_map/ppermute | solution.py:41
  66.3 4.4 %collective-permute-done.12.rest_1_ = bf16[128,2048]{1,0:T(8,128)(2,1)S(1)} collective-permute-done((bf16[128,2048]{1,0:T(8,128)(2,1)S(1)}, bf16[128,2048]{1,0:T(8,128)(2,1)S(1)}, u32[]{:S(2)}, u32[]{:S(2)}) %collective-permute-start.12) | collective-permute-done | bytes 524320 | tf_op jit(solution)/shard_map/ppermute | solution.py:41
  74.4 3.0 %collective-permute-start.16 = (bf16[128,2048]{1,0:T(8,128)(2,1)S(1)}, bf16[128,2048]{1,0:T(8,128)(2,1)S(1)}, u32[]{:S(2)}, u32[]{:S(2)}) collective-permute-start(bf16[128,2048]{1,0:T(8,128)(2,1)S(1)} %get-tuple-element.75), channel_id=1, source_target_pairs={{0,3},{1,0},{2,1},{3,2},{4,7},{5,4},{6,5},{7,6},{8,11},{9,8},{10,9... | collective-permute-start | bytes 1572872 | tf_op jit(solution)/shard_map/ppermute | solution.py:41
  77.5 4.5 %collective-permute-done.13.rest_0_ = bf16[128,2048]{1,0:T(8,128)(2,1)S(1)} collective-permute-done((bf16[128,2048]{1,0:T(8,128)(2,1)S(1)}, bf16[128,2048]{1,0:T(8,128)(2,1)S(1)}, u32[]{:S(2)}, u32[]{:S(2)}) %collective-permute-start.13) | collective-permute-done | bytes 524320 | tf_op jit(solution)/shard_map/ppermute | solution.py:41
  85.1 5.9 %collective-permute-done.16.rest_3_ = bf16[128,2048]{1,0:T(8,128)(2,1)S(1)} collective-permute-done((bf16[128,2048]{1,0:T(8,128)(2,1)S(1)}, bf16[128,2048]{1,0:T(8,128)(2,1)S(1)}, u32[]{:S(2)}, u32[]{:S(2)}) %collective-permute-start.16) | collective-permute-done | bytes 524320 | tf_op jit(solution)/shard_map/ppermute | solution.py:41
  102.4 4.3 %collective-permute-done.24.refs_5_.refs_1_.refs_6_.refs_9_ = bf16[1024,256]{1,0:T(8,128)(2,1)S(1)} collective-permute-done((bf16[1024,256]{1,0:T(8,128)(2,1)S(1)}, bf16[1024,256]{1,0:T(8,128)(2,1)S(1)}, u32[]{:S(2)}, u32[]{:S(2)}) %collective-permute-start.24) | collective-permute-done | bytes 524320 | tf_op jit(solution)/shard_map/ppermute | solution.py:41
  109.3 3.0 %collective-permute-start.28 = (bf16[128,2048]{1,0:T(8,128)(2,1)S(1)}, bf16[128,2048]{1,0:T(8,128)(2,1)S(1)}, u32[]{:S(2)}, u32[]{:S(2)}) collective-permute-start(bf16[128,2048]{1,0:T(8,128)(2,1)S(1)} %get-tuple-element.88), channel_id=1, source_target_pairs={{0,3},{1,0},{2,1},{3,2},{4,7},{5,4},{6,5},{7,6},{8,11},{9,8},{10,9... | collective-permute-start | bytes 1572872 | tf_op jit(solution)/shard_map/ppermute | solution.py:41
  119.0 6.3 %collective-permute-start.26 = (bf16[128,2048]{1,0:T(8,128)(2,1)S(1)}, bf16[128,2048]{1,0:T(8,128)(2,1)S(1)}, u32[]{:S(2)}, u32[]{:S(2)}) collective-permute-start(bf16[128,2048]{1,0:T(8,128)(2,1)S(1)} %get-tuple-element.86), channel_id=1, source_target_pairs={{0,3},{1,0},{2,1},{3,2},{4,7},{5,4},{6,5},{7,6},{8,11},{9,8},{10,9... | collective-permute-start | bytes 1572872 | tf_op jit(solution)/shard_map/ppermute | solution.py:41
  125.3 3.1 %shard_map.117 = (bf16[128,2048]{1,0:T(8,128)(2,1)S(1)}, bf16[128,2048]{1,0:T(8,128)(2,1)S(1)}) custom-call(s32[8]{0:T(128)S(1)} %stack.31.at, bf16[2,4,128,256]{3,2,1,0:T(8,128)(2,1)S(1)} %get-tuple-element.80.cot_ref, bf16[4,128,256]{2,1,0:T(8,128)(2,1)S(1)} %collective-permute-done.19.pair_ref, ...), custom_call_target="tpu_custom_call" | custom-call | flops 536870912 | bytes 10485760 | tf_op jit(solution)/shard_map/pallas_call | solution.py:73
  129.0 3.0 %collective-permute-start.31 = (bf16[128,2048]{1,0:T(8,128)(2,1)S(1)}, bf16[128,2048]{1,0:T(8,128)(2,1)S(1)}, u32[]{:S(2)}, u32[]{:S(2)}) collective-permute-start(bf16[128,2048]{1,0:T(8,128)(2,1)S(1)} %get-tuple-element.92), channel_id=1, source_target_pairs={{0,3},{1,0},{2,1},{3,2},{4,7},{5,4},{6,5},{7,6},{8,11},{9,8},{10,9... | collective-permute-start | bytes 1572872 | tf_op jit(solution)/shard_map/ppermute | solution.py:41
  132.0 2.9 %shard_map.112 = (bf16[128,4096]{1,0:T(8,128)(2,1)}, bf16[128,2048]{1,0:T(8,128)(2,1)S(1)}, bf16[128,2048]{1,0:T(8,128)(2,1)S(1)}, f32[128,1]{1,0:T(8,128)S(1)}) custom-call(s32[8]{0:T(128)S(1)} %stack.31.at, bf16[128,4096]{1,0:T(8,128)(2,1)S(1)} %collective-permute-done.r_ref, bf16[128,2048]{1,0:T(8,128)(2,1)S(1)} %collective-permute-done.9.k_ref, ...), custom_call_target="tpu_custom_call" | custom-call | flops 6291456 | bytes 4194304 | tf_op jit(solution)/shard_map/pallas_call | solution.py:73
  134.9 4.3 %collective-permute-start.41 = (bf16[128,2048]{1,0:T(8,128)(2,1)S(1)}, bf16[128,2048]{1,0:T(8,128)(2,1)S(1)}, u32[]{:S(2)}, u32[]{:S(2)}) collective-permute-start(bf16[128,2048]{1,0:T(8,128)(2,1)S(1)} %get-tuple-element.96.refs_0_), channel_id=1, source_target_pairs={{0,1},{1,2},{2,3},{3,0},{4,5},{5,6},{6,7},{7,4},{8,9},{9,10},{10,1... | collective-permute-start | bytes 1572872 | tf_op jit(solution)/shard_map/ppermute | solution.py:41
  141.3 4.2 %shard_map.114 = (f32[128,2048]{1,0:T(8,128)S(1)}, f32[128,2048]{1,0:T(8,128)S(1)}) custom-call(s32[8]{0:T(128)S(1)} %stack.31.at, bf16[2,4,128,256]{3,2,1,0:T(8,128)(2,1)S(1)} %get-tuple-element.80.cot_ref, bf16[4,128,256]{2,1,0:T(8,128)(2,1)S(1)} %collective-permute-done.19.pair_ref, bf16[1024,256]{1,0:T(8,128)(2,1)S(1)} %get-tuple-element.84.refs_0_.refs_6_.refs_2_, ...), custom_call_target="tpu_custom_call" | custom-call | flops 536870912 | bytes 8388608 | tf_op jit(solution)/shard_map/pallas_call | solution.py:73
  145.5 10.2 %collective-permute-done.29.h2 = bf16[128,2048]{1,0:T(8,128)(2,1)S(1)} collective-permute-done((bf16[128,2048]{1,0:T(8,128)(2,1)S(1)}, bf16[128,2048]{1,0:T(8,128)(2,1)S(1)}, u32[]{:S(2)}, u32[]{:S(2)}) %collective-permute-start.29) | collective-permute-done | bytes 524320 | tf_op jit(solution)/shard_map/ppermute | solution.py:41
  160.3 6.7 %collective-permute-done.41.refs_4_ = bf16[128,2048]{1,0:T(8,128)(2,1)S(1)} collective-permute-done((bf16[128,2048]{1,0:T(8,128)(2,1)S(1)}, bf16[128,2048]{1,0:T(8,128)(2,1)S(1)}, u32[]{:S(2)}, u32[]{:S(2)}) %collective-permute-start.41) | collective-permute-done | bytes 524320 | tf_op jit(solution)/shard_map/ppermute | solution.py:41
  166.9 3.2 %collective-permute-start.44 = (bf16[128,2048]{1,0:T(8,128)(2,1)S(1)}, bf16[128,2048]{1,0:T(8,128)(2,1)S(1)}, u32[]{:S(2)}, u32[]{:S(2)}) collective-permute-start(bf16[128,2048]{1,0:T(8,128)(2,1)S(1)} %collective-permute-done.40.refs_3_), channel_id=1, source_target_pairs={{0,3},{1,0},{2,1},{3,2},{4,7},{5,4},{6,5},{7,6},{8,11},{9,8},{10,9... | collective-permute-start | bytes 1572872 | tf_op jit(solution)/shard_map/ppermute | solution.py:41
  170.2 2.9 %collective-permute-done.39.refs_2_ = bf16[128,2048]{1,0:T(8,128)(2,1)S(1)} collective-permute-done((bf16[128,2048]{1,0:T(8,128)(2,1)S(1)}, bf16[128,2048]{1,0:T(8,128)(2,1)S(1)}, u32[]{:S(2)}, u32[]{:S(2)}) %collective-permute-start.39) | collective-permute-done | bytes 524320 | tf_op jit(solution)/shard_map/ppermute | solution.py:41
  173.0 5.1 %collective-permute-done.42.refs_5_ = bf16[128,2048]{1,0:T(8,128)(2,1)S(1)} collective-permute-done((bf16[128,2048]{1,0:T(8,128)(2,1)S(1)}, bf16[128,2048]{1,0:T(8,128)(2,1)S(1)}, u32[]{:S(2)}, u32[]{:S(2)}) %collective-permute-start.42) | collective-permute-done | bytes 524320 | tf_op jit(solution)/shard_map/ppermute | solution.py:41
  178.2 3.0 %shard_map.121 = (bf16[3,128,256]{2,1,0:T(8,128)(2,1)S(1)}, bf16[3,128,256]{2,1,0:T(8,128)(2,1)S(1)}) custom-call(s32[8]{0:T(128)S(1)} %stack.31.at, bf16[128,2048]{1,0:T(8,128)(2,1)S(1)} %get-tuple-element.96.refs_0_, bf16[128,2048]{1,0:T(8,128)(2,1)S(1)} %get-tuple-element.97.refs_1_, bf16[128,2048]{1,0:T(8,128)(2,1)S(1)} %collective-permute-done.39.refs_2_, ...), custom_call_target="tpu_custom_call" | custom-call | flops 1610612736 | bytes 7733248 | tf_op jit(solution)/shard_map/pallas_call | solution.py:73
  182.3 5.9 %collective-permute-done.43.refs_0_ = bf16[128,2048]{1,0:T(8,128)(2,1)S(1)} collective-permute-done((bf16[128,2048]{1,0:T(8,128)(2,1)S(1)}, bf16[128,2048]{1,0:T(8,128)(2,1)S(1)}, u32[]{:S(2)}, u32[]{:S(2)}) %collective-permute-start.43) | collective-permute-done | bytes 524320 | tf_op jit(solution)/shard_map/ppermute | solution.py:41
  191.4 3.9 %collective-permute-done.34.refs_2_ = f32[1,4096]{1,0:T(1,128)S(1)} collective-permute-done((f32[1,4096]{1,0:T(1,128)S(1)}, f32[1,4096]{1,0:T(1,128)S(1)}, u32[]{:S(2)}, u32[]{:S(2)}) %collective-permute-start.34) | collective-permute-done | bytes 16416 | tf_op jit(solution)/shard_map/ppermute | solution.py:41
  200.1 3.2 %collective-permute-start.36 = (f32[1,4096]{1,0:T(1,128)S(1)}, f32[1,4096]{1,0:T(1,128)S(1)}, u32[]{:S(2)}, u32[]{:S(2)}) collective-permute-start(f32[1,4096]{1,0:T(1,128)S(1)} %shard_map.119.refs_0_), channel_id=1, source_target_pairs={{0,8},{1,9},{2,10},{3,11},{4,12},{5,13},{6,14},{7,15},{8,0},{9,1},... | collective-permute-start | bytes 49160 | tf_op jit(solution)/shard_map/ppermute | solution.py:41
  (112 shorter events, 88.8 us)
Async XLA Ops:
  3.1 29.5 %collective-permute-start.3 = (bf16[4,128,1024]{2,1,0:T(8,128)(2,1)S(1)}, bf16[4,128,1024]{2,1,0:T(8,128)(2,1)S(1)}, u32[]{:S(2)}, u32[]{:S(2)}) collective-permute-start(bf16[4,128,1024]{2,1,0:T(8,128)(2,1)S(1)} %get-tuple-element.53.one_ref), channel_id=1, source_target_pairs={{0,8},{1,9},{2,10},{3,11},{4,12},{5,13},{6,14},{7,15},{8,0},{9,1},... | collective-permute-start | bytes 3145736 | tf_op jit(solution)/shard_map/ppermute | solution.py:41
  5.2 46.8 %collective-permute-start.4 = (bf16[4,128,1024]{2,1,0:T(8,128)(2,1)S(1)}, bf16[4,128,1024]{2,1,0:T(8,128)(2,1)S(1)}, u32[]{:S(2)}, u32[]{:S(2)}) collective-permute-start(bf16[4,128,1024]{2,1,0:T(8,128)(2,1)S(1)} %get-tuple-element.54.two_ref), channel_id=1, source_target_pairs={{0,8},{1,9},{2,10},{3,11},{4,12},{5,13},{6,14},{7,15},{8,0},{9,1},... | collective-permute-start | bytes 3145736 | tf_op jit(solution)/shard_map/ppermute | solution.py:41
  16.5 39.4 %collective-permute-start.7 = (bf16[128,2048]{1,0:T(8,128)(2,1)S(1)}, bf16[128,2048]{1,0:T(8,128)(2,1)S(1)}, u32[]{:S(2)}, u32[]{:S(2)}) collective-permute-start(bf16[128,2048]{1,0:T(8,128)(2,1)S(1)} %get-tuple-element.66), channel_id=1, source_target_pairs={{0,1},{1,2},{2,3},{3,0},{4,5},{5,6},{6,7},{7,4},{8,9},{9,10},{10,1... | collective-permute-start | bytes 1572872 | tf_op jit(solution)/shard_map/ppermute | solution.py:41
  24.7 33.7 %collective-permute-start.5 = (bf16[128,2048]{1,0:T(8,128)(2,1)S(1)}, bf16[128,2048]{1,0:T(8,128)(2,1)S(1)}, u32[]{:S(2)}, u32[]{:S(2)}) collective-permute-start(bf16[128,2048]{1,0:T(8,128)(2,1)S(1)} %get-tuple-element.57), channel_id=1, source_target_pairs={{0,3},{1,0},{2,1},{3,2},{4,7},{5,4},{6,5},{7,6},{8,11},{9,8},{10,9... | collective-permute-start | bytes 1572872 | tf_op jit(solution)/shard_map/ppermute | solution.py:41
  32.5 26.5 %collective-permute-start.8 = (bf16[128,2048]{1,0:T(8,128)(2,1)S(1)}, bf16[128,2048]{1,0:T(8,128)(2,1)S(1)}, u32[]{:S(2)}, u32[]{:S(2)}) collective-permute-start(bf16[128,2048]{1,0:T(8,128)(2,1)S(1)} %get-tuple-element.67), channel_id=1, source_target_pairs={{0,3},{1,0},{2,1},{3,2},{4,7},{5,4},{6,5},{7,6},{8,11},{9,8},{10,9... | collective-permute-start | bytes 1572872 | tf_op jit(solution)/shard_map/ppermute | solution.py:41
  32.6 28.0 %collective-permute-start.6 = (bf16[128,2048]{1,0:T(8,128)(2,1)S(1)}, bf16[128,2048]{1,0:T(8,128)(2,1)S(1)}, u32[]{:S(2)}, u32[]{:S(2)}) collective-permute-start(bf16[128,2048]{1,0:T(8,128)(2,1)S(1)} %get-tuple-element.60), channel_id=1, source_target_pairs={{0,1},{1,2},{2,3},{3,0},{4,5},{5,6},{6,7},{7,4},{8,9},{9,10},{10,1... | collective-permute-start | bytes 1572872 | tf_op jit(solution)/shard_map/ppermute | solution.py:41
  58.5 19.0 %collective-permute-start.23 = (bf16[1024,256]{1,0:T(8,128)(2,1)S(1)}, bf16[1024,256]{1,0:T(8,128)(2,1)S(1)}, u32[]{:S(2)}, u32[]{:S(2)}) collective-permute-start(bf16[1024,256]{1,0:T(8,128)(2,1)S(1)} %get-tuple-element.83.refs_1_.refs_7_.refs_3_), channel_id=1, source_target_pairs={{0,12},{1,13},{2,14},{3,15},{4,8},{5,9},{6,10},{7,11},{8,4},{9,5},... | collective-permute-start | bytes 1572872 | tf_op jit(solution)/shard_map/ppermute | solution.py:41
  59.0 23.0 %collective-permute-start.13 = (bf16[128,2048]{1,0:T(8,128)(2,1)S(1)}, bf16[128,2048]{1,0:T(8,128)(2,1)S(1)}, u32[]{:S(2)}, u32[]{:S(2)}) collective-permute-start(bf16[128,2048]{1,0:T(8,128)(2,1)S(1)} %get-tuple-element.73), channel_id=1, source_target_pairs={{0,3},{1,0},{2,1},{3,2},{4,7},{5,4},{6,5},{7,6},{8,11},{9,8},{10,9... | collective-permute-start | bytes 1572872 | tf_op jit(solution)/shard_map/ppermute | solution.py:41
  66.1 17.2 %collective-permute-start.15 = (bf16[128,2048]{1,0:T(8,128)(2,1)S(1)}, bf16[128,2048]{1,0:T(8,128)(2,1)S(1)}, u32[]{:S(2)}, u32[]{:S(2)}) collective-permute-start(bf16[128,2048]{1,0:T(8,128)(2,1)S(1)} %get-tuple-element.74), channel_id=1, source_target_pairs={{0,1},{1,2},{2,3},{3,0},{4,5},{5,6},{6,7},{7,4},{8,9},{9,10},{10,1... | collective-permute-start | bytes 1572872 | tf_op jit(solution)/shard_map/ppermute | solution.py:41
  83.3 17.5 %collective-permute-start.25 = (bf16[1024,256]{1,0:T(8,128)(2,1)S(1)}, bf16[1024,256]{1,0:T(8,128)(2,1)S(1)}, u32[]{:S(2)}, u32[]{:S(2)}) collective-permute-start(bf16[1024,256]{1,0:T(8,128)(2,1)S(1)} %get-tuple-element.84.refs_0_.refs_6_.refs_2_), channel_id=1, source_target_pairs={{0,12},{1,13},{2,14},{3,15},{4,8},{5,9},{6,10},{7,11},{8,4},{9,5},... | collective-permute-start | bytes 1572872 | tf_op jit(solution)/shard_map/ppermute | solution.py:41
  83.3 23.3 %collective-permute-start.24 = (bf16[1024,256]{1,0:T(8,128)(2,1)S(1)}, bf16[1024,256]{1,0:T(8,128)(2,1)S(1)}, u32[]{:S(2)}, u32[]{:S(2)}) collective-permute-start(bf16[1024,256]{1,0:T(8,128)(2,1)S(1)} %collective-permute-done.23.refs_7_.refs_3_.refs_8_.refs_13_.refs_9_), channel_id=1, source_target_pairs={{0,4},{1,5},{2,6},{3,7},{4,0},{5,1},{6,2},{7,3},{8,12},{9,13},{10,... | collective-permute-start | bytes 1572872 | tf_op jit(solution)/shard_map/ppermute | solution.py:41
  91.4 36.9 %collective-permute-start = (bf16[128,4096]{1,0:T(8,128)(2,1)S(1)}, bf16[128,4096]{1,0:T(8,128)(2,1)S(1)}, u32[]{:S(2)}, u32[]{:S(2)}) collective-permute-start(bf16[128,4096]{1,0:T(8,128)(2,1)S(1)} %bitcast.31), channel_id=1, source_target_pairs={{0,16},{1,17},{2,18},{3,19},{4,20},{5,21},{6,22},{7,23},{8,24},{9,... | collective-permute-start | bytes 3145736 | tf_op jit(solution)/shard_map/ppermute | solution.py:52
  96.8 17.1 %collective-permute-start.17 = (bf16[128,2048]{1,0:T(8,128)(2,1)S(1)}, bf16[128,2048]{1,0:T(8,128)(2,1)S(1)}, u32[]{:S(2)}, u32[]{:S(2)}) collective-permute-start(bf16[128,2048]{1,0:T(8,128)(2,1)S(1)} %get-tuple-element.77), channel_id=1, source_target_pairs={{0,4},{1,5},{2,6},{3,7},{4,0},{5,1},{6,2},{7,3},{8,12},{9,13},{10,... | collective-permute-start | bytes 1572872 | tf_op jit(solution)/shard_map/ppermute | solution.py:41
  119.0 20.2 %collective-permute-start.26 = (bf16[128,2048]{1,0:T(8,128)(2,1)S(1)}, bf16[128,2048]{1,0:T(8,128)(2,1)S(1)}, u32[]{:S(2)}, u32[]{:S(2)}) collective-permute-start(bf16[128,2048]{1,0:T(8,128)(2,1)S(1)} %get-tuple-element.86), channel_id=1, source_target_pairs={{0,3},{1,0},{2,1},{3,2},{4,7},{5,4},{6,5},{7,6},{8,11},{9,8},{10,9... | collective-permute-start | bytes 1572872 | tf_op jit(solution)/shard_map/ppermute | solution.py:41
  128.5 27.2 %collective-permute-start.29 = (bf16[128,2048]{1,0:T(8,128)(2,1)S(1)}, bf16[128,2048]{1,0:T(8,128)(2,1)S(1)}, u32[]{:S(2)}, u32[]{:S(2)}) collective-permute-start(bf16[128,2048]{1,0:T(8,128)(2,1)S(1)} %get-tuple-element.89), channel_id=1, source_target_pairs={{0,1},{1,2},{2,3},{3,0},{4,5},{5,6},{6,7},{7,4},{8,9},{9,10},{10,1... | collective-permute-start | bytes 1572872 | tf_op jit(solution)/shard_map/ppermute | solution.py:41
  129.0 26.7 %collective-permute-start.31 = (bf16[128,2048]{1,0:T(8,128)(2,1)S(1)}, bf16[128,2048]{1,0:T(8,128)(2,1)S(1)}, u32[]{:S(2)}, u32[]{:S(2)}) collective-permute-start(bf16[128,2048]{1,0:T(8,128)(2,1)S(1)} %get-tuple-element.92), channel_id=1, source_target_pairs={{0,3},{1,0},{2,1},{3,2},{4,7},{5,4},{6,5},{7,6},{8,11},{9,8},{10,9... | collective-permute-start | bytes 1572872 | tf_op jit(solution)/shard_map/ppermute | solution.py:41
  134.9 32.1 %collective-permute-start.41 = (bf16[128,2048]{1,0:T(8,128)(2,1)S(1)}, bf16[128,2048]{1,0:T(8,128)(2,1)S(1)}, u32[]{:S(2)}, u32[]{:S(2)}) collective-permute-start(bf16[128,2048]{1,0:T(8,128)(2,1)S(1)} %get-tuple-element.96.refs_0_), channel_id=1, source_target_pairs={{0,1},{1,2},{2,3},{3,0},{4,5},{5,6},{6,7},{7,4},{8,9},{9,10},{10,1... | collective-permute-start | bytes 1572872 | tf_op jit(solution)/shard_map/ppermute | solution.py:41
  139.2 27.7 %collective-permute-start.40 = (bf16[128,2048]{1,0:T(8,128)(2,1)S(1)}, bf16[128,2048]{1,0:T(8,128)(2,1)S(1)}, u32[]{:S(2)}, u32[]{:S(2)}) collective-permute-start(bf16[128,2048]{1,0:T(8,128)(2,1)S(1)} %get-tuple-element.97.refs_1_), channel_id=1, source_target_pairs={{0,3},{1,0},{2,1},{3,2},{4,7},{5,4},{6,5},{7,6},{8,11},{9,8},{10,9... | collective-permute-start | bytes 1572872 | tf_op jit(solution)/shard_map/ppermute | solution.py:41
  158.1 48.3 %collective-permute-start.32 = (bf16[128,4096]{1,0:T(8,128)(2,1)S(1)}, bf16[128,4096]{1,0:T(8,128)(2,1)S(1)}, u32[]{:S(2)}, u32[]{:S(2)}) collective-permute-start(bf16[128,4096]{1,0:T(8,128)(2,1)S(1)} %get-tuple-element.93), channel_id=1, source_target_pairs={{0,240},{1,241},{2,242},{3,243},{4,244},{5,245},{6,246},{7,247},{8... | collective-permute-start | bytes 3145736 | tf_op jit(solution)/shard_map/ppermute | solution.py:52
  158.2 19.9 %collective-permute-start.42 = (bf16[128,2048]{1,0:T(8,128)(2,1)S(1)}, bf16[128,2048]{1,0:T(8,128)(2,1)S(1)}, u32[]{:S(2)}, u32[]{:S(2)}) collective-permute-start(bf16[128,2048]{1,0:T(8,128)(2,1)S(1)} %get-tuple-element.97.refs_1_), channel_id=1, source_target_pairs={{0,1},{1,2},{2,3},{3,0},{4,5},{5,6},{6,7},{7,4},{8,9},{9,10},{10,1... | collective-permute-start | bytes 1572872 | tf_op jit(solution)/shard_map/ppermute | solution.py:41
  166.9 21.3 %collective-permute-start.43 = (bf16[128,2048]{1,0:T(8,128)(2,1)S(1)}, bf16[128,2048]{1,0:T(8,128)(2,1)S(1)}, u32[]{:S(2)}, u32[]{:S(2)}) collective-permute-start(bf16[128,2048]{1,0:T(8,128)(2,1)S(1)} %collective-permute-done.41.refs_4_), channel_id=1, source_target_pairs={{0,1},{1,2},{2,3},{3,0},{4,5},{5,6},{6,7},{7,4},{8,9},{9,10},{10,1... | collective-permute-start | bytes 1572872 | tf_op jit(solution)/shard_map/ppermute | solution.py:41
  166.9 21.3 %collective-permute-start.44 = (bf16[128,2048]{1,0:T(8,128)(2,1)S(1)}, bf16[128,2048]{1,0:T(8,128)(2,1)S(1)}, u32[]{:S(2)}, u32[]{:S(2)}) collective-permute-start(bf16[128,2048]{1,0:T(8,128)(2,1)S(1)} %collective-permute-done.40.refs_3_), channel_id=1, source_target_pairs={{0,3},{1,0},{2,1},{3,2},{4,7},{5,4},{6,5},{7,6},{8,11},{9,8},{10,9... | collective-permute-start | bytes 1572872 | tf_op jit(solution)/shard_map/ppermute | solution.py:41
  181.1 26.3 %collective-permute-start.45 = (bf16[3,128,256]{2,1,0:T(8,128)(2,1)S(1)}, bf16[3,128,256]{2,1,0:T(8,128)(2,1)S(1)}, u32[]{:S(2)}, u32[]{:S(2)}) collective-permute-start(bf16[3,128,256]{2,1,0:T(8,128)(2,1)S(1)} %get-tuple-element.100), channel_id=1, source_target_pairs={{0,4},{1,5},{2,6},{3,7},{4,0},{5,1},{6,2},{7,3},{8,12},{9,13},{10,... | collective-permute-start | bytes 589832 | tf_op jit(solution)/shard_map/ppermute | solution.py:41
  189.5 18.0 %collective-permute-start.46 = (bf16[1,128,256]{2,1,0:T(8,128)(2,1)S(1)}, bf16[1,128,256]{2,1,0:T(8,128)(2,1)S(1)}, u32[]{:S(2)}, u32[]{:S(2)}) collective-permute-start(bf16[1,128,256]{2,1,0:T(8,128)(2,1)S(1)} %get-tuple-element.101), channel_id=1, source_target_pairs={{0,4},{1,5},{2,6},{3,7},{4,0},{5,1},{6,2},{7,3},{8,12},{9,13},{10,... | collective-permute-start | bytes 196616 | tf_op jit(solution)/shard_map/ppermute | solution.py:41
  (32 other events, 445.1 us)
